TPU v7x, 32 devices: a whole 2x2x4 slice. The times are simulated.
32 devices in a mesh: dp: 4 (over x, core), mem: 8 (over z, y).
Axes of the slice: x: 2, y: 2, z: 4, core: 2. Of those that a mesh axis runs over, the one named last changes fastest.
Arguments:
- text: bfloat16 [256, 64, 768], P(('dp', 'mem')), may hold values from -6 to 6
- lengths: int32 [256], P(('dp', 'mem')), may hold values from 1 to 64, as said below
- memory: bfloat16 [256, 96, 768], P('dp', 'mem'), may hold values from -6 to 6
- out_grad: bfloat16 [256, 64, 768], P(('dp', 'mem')), may hold values from -6 to 6
- self_query: bfloat16 [768, 768], P('dp', 'mem'), may hold values from -0.21875 to 0.21875
- self_key: bfloat16 [768, 768], P('dp', 'mem'), may hold values from -0.21875 to 0.21875
- self_value: bfloat16 [768, 768], P('dp', 'mem'), may hold values from -0.21875 to 0.21875
- self_output: bfloat16 [768, 768], P('dp', 'mem'), may hold values from -0.5 to 0.5
- cross_query: bfloat16 [768, 768], P('dp', 'mem'), may hold values from -0.21875 to 0.21875
- cross_key: bfloat16 [768, 768], P('dp', 'mem'), may hold values from -0.21875 to 0.21875
- cross_value: bfloat16 [768, 768], P('dp', 'mem'), may hold values from -0.21875 to 0.21875
- cross_output: bfloat16 [768, 768], P('dp', 'mem'), may hold values from -0.75 to 0.75
- hidden_in: bfloat16 [768, 3072], P('dp', 'mem'), may hold values from -0.21875 to 0.21875
- hidden_out: bfloat16 [3072, 768], P('dp', 'mem'), may hold values from -0.109375 to 0.109375
- first_gain: float32 [768], replicated, may hold values from 0.5 to 1.5
- first_shift: float32 [768], replicated, may hold values from -3 to 3
- second_gain: float32 [768], replicated, may hold values from 0.5 to 1.5
- second_shift: float32 [768], replicated, may hold values from -3 to 3
- third_gain: float32 [768], replicated, may hold values from 0.5 to 1.5
- third_shift: float32 [768], replicated, may hold values from -3 to 3
Outputs:
- layer_out: bfloat16 [256, 64, 768], P(('dp', 'mem'))
- text_grad: bfloat16 [256, 64, 768], P(('dp', 'mem'))
- memory_grad: bfloat16 [256, 96, 768], P('dp', 'mem')
- self_query_grad: float32 [768, 768], P('dp', 'mem')
- self_key_grad: float32 [768, 768], P('dp', 'mem')
- self_value_grad: float32 [768, 768], P('dp', 'mem')
- self_output_grad: float32 [768, 768], P('dp', 'mem')
- cross_query_grad: float32 [768, 768], P('dp', 'mem')
- cross_key_grad: float32 [768, 768], P('dp', 'mem')
- cross_value_grad: float32 [768, 768], P('dp', 'mem')
- cross_output_grad: float32 [768, 768], P('dp', 'mem')
- hidden_in_grad: float32 [768, 3072], P('dp', 'mem')
- hidden_out_grad: float32 [3072, 768], P('dp', 'mem')
- first_gain_grad: float32 [768], replicated
- first_shift_grad: float32 [768], replicated
- second_gain_grad: float32 [768], replicated
- second_shift_grad: float32 [768], replicated
- third_gain_grad: float32 [768], replicated
- third_shift_grad: float32 [768], replicated
Inputs may be any that keep to these rules, and one draw needn't show every extreme that they name: `lengths`: each image's caption length; slots at and beyond it are padding; some image has 64 and some has 1.
All inputs are finite; a program needn't handle non-finite values.
Results may differ from a plain program's by a relative error of at most 0.023.
Values may be sent and summed in bfloat16 or wider, within the bound.
A program may use at most 192 MiB of HBM per device.

v0:
```python
import jax
import jax.numpy as jnp
from jax import lax
from jax.sharding import PartitionSpec as P

HEADS = 12
HEAD = 64


EPS = 1e-06
NEG = -1e30


def layer_norm(values, scaling, offsets):
    center = values - jnp.mean(values, axis=-1, keepdims=True)
    spread = jnp.mean(center * center, axis=-1, keepdims=True)
    return center * lax.rsqrt(spread + EPS) * scaling + offsets


def norm_back(values, scaling, offsets, upstream):
    _, pull_back = jax.vjp(layer_norm, values, scaling, offsets)
    return pull_back(upstream)


def split_heads(values):
    return values.reshape(values.shape[0], values.shape[1], HEADS, HEAD)


def join_heads(values):
    return values.reshape(values.shape[0], values.shape[1], HEADS * HEAD)


def apply_mat(acts, matrix):
    return jnp.einsum("bsd,de->bse", acts, matrix, preferred_element_type=jnp.float32)


def apply_back(grads, matrix):
    return jnp.einsum("bse,de->bsd", grads, matrix, preferred_element_type=jnp.float32)


def mat_grad(acts, grads):
    return jnp.einsum("bsd,bse->de", acts, grads, preferred_element_type=jnp.float32)


def score_rows(queries, keys, allowed):
    score_scale = HEAD ** (-0.5)
    scores = (
        jnp.einsum(
            "bshd,bthd->bhst",
            split_heads(queries),
            split_heads(keys),
            preferred_element_type=jnp.float32,
        )
        * score_scale
    )
    if allowed is not None:
        scores = jnp.where(allowed, scores, NEG)
    return scores


def attend_fwd(queries, keys, values, allowed):
    scores = score_rows(queries, keys, allowed)
    highest = jnp.max(scores, axis=-1, keepdims=True)
    powered = jnp.exp(scores - highest)
    expo_sum = jnp.sum(powered, axis=-1, keepdims=True)
    weights = (powered / expo_sum).astype(jnp.bfloat16)
    mixed_heads = jnp.einsum(
        "bhst,bthd->bshd", weights, split_heads(values), preferred_element_type=jnp.float32
    )
    return (join_heads(mixed_heads).astype(jnp.bfloat16), highest + jnp.log(expo_sum))


def attend_back(queries, keys, values, allowed, log_sum, upstream):
    score_scale = HEAD ** (-0.5)
    probs_full = jnp.exp(score_rows(queries, keys, allowed) - log_sum)
    heads_up = split_heads(upstream)
    prob_grad = jnp.einsum(
        "bshd,bthd->bhst", heads_up, split_heads(values), preferred_element_type=jnp.float32
    )
    score_low = (
        probs_full * (prob_grad - jnp.sum(prob_grad * probs_full, axis=-1, keepdims=True))
    ).astype(jnp.bfloat16)
    value_grad = jnp.einsum(
        "bhst,bshd->bthd",
        probs_full.astype(jnp.bfloat16),
        heads_up,
        preferred_element_type=jnp.float32,
    )
    query_grad = (
        jnp.einsum(
            "bhst,bthd->bshd", score_low, split_heads(keys), preferred_element_type=jnp.float32
        )
        * score_scale
    )
    key_grad = (
        jnp.einsum(
            "bhst,bshd->bthd", score_low, split_heads(queries), preferred_element_type=jnp.float32
        )
        * score_scale
    )
    return (
        join_heads(query_grad).astype(jnp.bfloat16),
        join_heads(key_grad).astype(jnp.bfloat16),
        join_heads(value_grad).astype(jnp.bfloat16),
    )


def fetch_weights(mats):
    columns = (
        lax.all_gather(mats[0], "mem", axis=1, tiled=True),
        lax.all_gather(mats[1], "mem", axis=1, tiled=True),
        lax.all_gather(mats[2], "mem", axis=1, tiled=True),
        lax.all_gather(mats[3], "mem", axis=1, tiled=True),
        lax.all_gather(mats[4], "mem", axis=1, tiled=True),
        lax.all_gather(mats[5], "mem", axis=1, tiled=True),
        lax.all_gather(mats[6], "mem", axis=1, tiled=True),
        lax.all_gather(mats[7], "mem", axis=1, tiled=True),
        lax.all_gather(mats[8], "mem", axis=1, tiled=True),
        lax.all_gather(mats[9], "mem", axis=1, tiled=True),
    )
    return (
        lax.all_gather(columns[0], "dp", axis=0, tiled=True),
        lax.all_gather(columns[1], "dp", axis=0, tiled=True),
        lax.all_gather(columns[2], "dp", axis=0, tiled=True),
        lax.all_gather(columns[3], "dp", axis=0, tiled=True),
        lax.all_gather(columns[4], "dp", axis=0, tiled=True),
        lax.all_gather(columns[5], "dp", axis=0, tiled=True),
        lax.all_gather(columns[6], "dp", axis=0, tiled=True),
        lax.all_gather(columns[7], "dp", axis=0, tiled=True),
        lax.all_gather(columns[8], "dp", axis=0, tiled=True),
        lax.all_gather(columns[9], "dp", axis=0, tiled=True),
    )


def reduce_all(grads):
    row_sums = (
        lax.psum_scatter(
            grads[0].astype(jnp.bfloat16), "dp", scatter_dimension=0, tiled=True
        ).astype(jnp.float32),
        lax.psum_scatter(
            grads[1].astype(jnp.bfloat16), "dp", scatter_dimension=0, tiled=True
        ).astype(jnp.float32),
        lax.psum_scatter(
            grads[2].astype(jnp.bfloat16), "dp", scatter_dimension=0, tiled=True
        ).astype(jnp.float32),
        lax.psum_scatter(
            grads[3].astype(jnp.bfloat16), "dp", scatter_dimension=0, tiled=True
        ).astype(jnp.float32),
        lax.psum_scatter(
            grads[4].astype(jnp.bfloat16), "dp", scatter_dimension=0, tiled=True
        ).astype(jnp.float32),
        lax.psum_scatter(
            grads[5].astype(jnp.bfloat16), "dp", scatter_dimension=0, tiled=True
        ).astype(jnp.float32),
        lax.psum_scatter(
            grads[6].astype(jnp.bfloat16), "dp", scatter_dimension=0, tiled=True
        ).astype(jnp.float32),
        lax.psum_scatter(
            grads[7].astype(jnp.bfloat16), "dp", scatter_dimension=0, tiled=True
        ).astype(jnp.float32),
        lax.psum_scatter(
            grads[8].astype(jnp.bfloat16), "dp", scatter_dimension=0, tiled=True
        ).astype(jnp.float32),
        lax.psum_scatter(
            grads[9].astype(jnp.bfloat16), "dp", scatter_dimension=0, tiled=True
        ).astype(jnp.float32),
    )
    return (
        lax.psum_scatter(
            row_sums[0].astype(jnp.bfloat16), "mem", scatter_dimension=1, tiled=True
        ).astype(jnp.float32),
        lax.psum_scatter(
            row_sums[1].astype(jnp.bfloat16), "mem", scatter_dimension=1, tiled=True
        ).astype(jnp.float32),
        lax.psum_scatter(
            row_sums[2].astype(jnp.bfloat16), "mem", scatter_dimension=1, tiled=True
        ).astype(jnp.float32),
        lax.psum_scatter(
            row_sums[3].astype(jnp.bfloat16), "mem", scatter_dimension=1, tiled=True
        ).astype(jnp.float32),
        lax.psum_scatter(
            row_sums[4].astype(jnp.bfloat16), "mem", scatter_dimension=1, tiled=True
        ).astype(jnp.float32),
        lax.psum_scatter(
            row_sums[5].astype(jnp.bfloat16), "mem", scatter_dimension=1, tiled=True
        ).astype(jnp.float32),
        lax.psum_scatter(
            row_sums[6].astype(jnp.bfloat16), "mem", scatter_dimension=1, tiled=True
        ).astype(jnp.float32),
        lax.psum_scatter(
            row_sums[7].astype(jnp.bfloat16), "mem", scatter_dimension=1, tiled=True
        ).astype(jnp.float32),
        lax.psum_scatter(
            row_sums[8].astype(jnp.bfloat16), "mem", scatter_dimension=1, tiled=True
        ).astype(jnp.float32),
        lax.psum_scatter(
            row_sums[9].astype(jnp.bfloat16), "mem", scatter_dimension=1, tiled=True
        ).astype(jnp.float32),
    )


def shards(
    text,
    lengths,
    memory,
    out_grad,
    self_query,
    self_key,
    self_value,
    self_output,
    cross_query,
    cross_key,
    cross_value,
    cross_output,
    hidden_in,
    hidden_out,
    first_gain,
    first_shift,
    second_gain,
    second_shift,
    third_gain,
    third_shift,
):
    mats = (
        self_query,
        self_key,
        self_value,
        self_output,
        cross_query,
        cross_key,
        cross_value,
        cross_output,
        hidden_in,
        hidden_out,
    )
    full_mats = fetch_weights(mats)
    w_query, w_key, w_value, w_output, m_query, m_key, m_value, m_output, w_in, w_out = full_mats
    places = jnp.arange(text.shape[1])
    valid_row = places[None, :] < lengths[:, None]
    allowed = (places[None, :] <= places[:, None])[None, None] & valid_row[:, None, None, :]
    residual = text.astype(jnp.float32)
    first = layer_norm(residual, first_gain, first_shift).astype(jnp.bfloat16)
    queries = apply_mat(first, w_query).astype(jnp.bfloat16)
    keys = apply_mat(first, w_key).astype(jnp.bfloat16)
    values = apply_mat(first, w_value).astype(jnp.bfloat16)
    self_mixed, self_lse = attend_fwd(queries, keys, values, allowed)
    after_self = residual + apply_mat(self_mixed, w_output)
    memory_rows = lax.all_to_all(memory, "mem", split_axis=0, concat_axis=1, tiled=True)
    second = layer_norm(after_self, second_gain, second_shift).astype(jnp.bfloat16)
    cross_queries = apply_mat(second, m_query).astype(jnp.bfloat16)
    mem_keys = apply_mat(memory_rows, m_key).astype(jnp.bfloat16)
    mem_values = apply_mat(memory_rows, m_value).astype(jnp.bfloat16)
    cross_mixed, cross_lse = attend_fwd(cross_queries, mem_keys, mem_values, None)
    after_cross = after_self + apply_mat(cross_mixed, m_output)
    third = layer_norm(after_cross, third_gain, third_shift).astype(jnp.bfloat16)
    before_act = apply_mat(third, w_in)
    activated = jax.nn.gelu(before_act).astype(jnp.bfloat16)
    final = after_cross + apply_mat(activated, w_out)
    layer_out = jnp.where(valid_row[:, :, None], final, 0.0).astype(jnp.bfloat16)
    b_query, b_key, b_value, b_output, n_query, n_key, n_value, n_output, b_in, b_out = full_mats
    grad_top = jnp.where(valid_row[:, :, None], out_grad.astype(jnp.float32), 0.0)
    top_low = grad_top.astype(jnp.bfloat16)
    hidden_out_grad = mat_grad(activated, top_low)
    _, gelu_pull = jax.vjp(jax.nn.gelu, before_act)
    act_low = gelu_pull(apply_back(top_low, b_out))[0].astype(jnp.bfloat16)
    hidden_in_grad = mat_grad(third, act_low)
    cross_input, third_gain_grad, third_shift_grad = norm_back(
        after_cross, third_gain, third_shift, apply_back(act_low, b_in)
    )
    grad_cross = grad_top + cross_input
    cross_low = grad_cross.astype(jnp.bfloat16)
    cross_output_grad = mat_grad(cross_mixed, cross_low)
    mixed_up = apply_back(cross_low, n_output).astype(jnp.bfloat16)
    cross_query_low, mem_key_low, mem_value_low = attend_back(
        cross_queries, mem_keys, mem_values, None, cross_lse, mixed_up
    )
    cross_query_grad = mat_grad(second, cross_query_low)
    cross_key_grad = mat_grad(memory_rows, mem_key_low)
    cross_value_grad = mat_grad(memory_rows, mem_value_low)
    mem_back = (apply_back(mem_key_low, n_key) + apply_back(mem_value_low, n_value)).astype(
        jnp.bfloat16
    )
    memory_grad = lax.all_to_all(mem_back, "mem", split_axis=1, concat_axis=0, tiled=True)
    self_input, second_gain_grad, second_shift_grad = norm_back(
        after_self, second_gain, second_shift, apply_back(cross_query_low, n_query)
    )
    grad_self = grad_cross + self_input
    self_low = grad_self.astype(jnp.bfloat16)
    self_output_grad = mat_grad(self_mixed, self_low)
    self_up = apply_back(self_low, b_output).astype(jnp.bfloat16)
    query_low, key_low, value_low = attend_back(queries, keys, values, allowed, self_lse, self_up)
    self_query_grad = mat_grad(first, query_low)
    self_key_grad = mat_grad(first, key_low)
    self_value_grad = mat_grad(first, value_low)
    first_up = (
        apply_back(query_low, b_query) + apply_back(key_low, b_key) + apply_back(value_low, b_value)
    )
    text_input, first_gain_grad, first_shift_grad = norm_back(
        residual, first_gain, first_shift, first_up
    )
    text_grad = (grad_self + text_input).astype(jnp.bfloat16)
    weight_sums = reduce_all(
        (
            self_query_grad,
            self_key_grad,
            self_value_grad,
            self_output_grad,
            cross_query_grad,
            cross_key_grad,
            cross_value_grad,
            cross_output_grad,
            hidden_in_grad,
            hidden_out_grad,
        )
    )
    norm_sums = lax.psum(
        (
            first_gain_grad,
            first_shift_grad,
            second_gain_grad,
            second_shift_grad,
            third_gain_grad,
            third_shift_grad,
        ),
        ("dp", "mem"),
    )
    return (
        layer_out,
        text_grad,
        memory_grad,
        weight_sums[0],
        weight_sums[1],
        weight_sums[2],
        weight_sums[3],
        weight_sums[4],
        weight_sums[5],
        weight_sums[6],
        weight_sums[7],
        weight_sums[8],
        weight_sums[9],
        norm_sums[0],
        norm_sums[1],
        norm_sums[2],
        norm_sums[3],
        norm_sums[4],
        norm_sums[5],
    )


def solution(mesh):
    return jax.shard_map(
        shards,
        mesh=mesh,
        in_specs=(
            P(("dp", "mem"), None, None),
            P(("dp", "mem")),
            P("dp", "mem", None),
            P(("dp", "mem"), None, None),
            P("dp", "mem"),
            P("dp", "mem"),
            P("dp", "mem"),
            P("dp", "mem"),
            P("dp", "mem"),
            P("dp", "mem"),
            P("dp", "mem"),
            P("dp", "mem"),
            P("dp", "mem"),
            P("dp", "mem"),
            P(),
            P(),
            P(),
            P(),
            P(),
            P(),
        ),
        out_specs=(
            P(("dp", "mem"), None, None),
            P(("dp", "mem"), None, None),
            P("dp", "mem", None),
            P("dp", "mem"),
            P("dp", "mem"),
            P("dp", "mem"),
            P("dp", "mem"),
            P("dp", "mem"),
            P("dp", "mem"),
            P("dp", "mem"),
            P("dp", "mem"),
            P("dp", "mem"),
            P("dp", "mem"),
            P(),
            P(),
            P(),
            P(),
            P(),
            P(),
        ),
        check_vma=False,
    )
```

profile of v0, /device:TPU:0, one launch (start us, length us, event | category | flops | bytes accessed | tf_op | source)
XLA Modules:
  0.0 1362.6 jit_solution(17380204440396111989)
XLA Ops:
  9.6 33.3 %all_gather.62 = bf16[192,768]{0,1:T(8,128)(2,1)S(1)} all-gather(bf16[192,96]{0,1:T(8,128)(2,1)S(1)} %copy.168), channel_id=1, replica_groups=mesh['dp'=4,'mem'=8] {'mem'}, dimensions={1}, use_global_device_ids=true | all-gather | bytes 331776 | tf_op jit(solution)/shard_map/all_gather | solution.py:110
  44.0 31.8 %all_gather.64 = bf16[192,768]{0,1:T(8,128)(2,1)S(1)} all-gather(bf16[192,96]{0,1:T(8,128)(2,1)S(1)} %copy.170), channel_id=1, replica_groups=mesh['dp'=4,'mem'=8] {'mem'}, dimensions={1}, use_global_device_ids=true | all-gather | bytes 331776 | tf_op jit(solution)/shard_map/all_gather | solution.py:111
  76.9 31.7 %all_gather.60 = bf16[192,768]{0,1:T(8,128)(2,1)S(1)} all-gather(bf16[192,96]{0,1:T(8,128)(2,1)S(1)} %copy.166), channel_id=1, replica_groups=mesh['dp'=4,'mem'=8] {'mem'}, dimensions={1}, use_global_device_ids=true | all-gather | bytes 331776 | tf_op jit(solution)/shard_map/all_gather | solution.py:112
  109.7 31.0 %all_gather.66 = bf16[192,768]{0,1:T(8,128)(2,1)S(1)} all-gather(bf16[192,96]{0,1:T(8,128)(2,1)S(1)} %copy.176), channel_id=1, replica_groups=mesh['dp'=4,'mem'=8] {'mem'}, dimensions={1}, use_global_device_ids=true | all-gather | bytes 331776 | tf_op jit(solution)/shard_map/all_gather | solution.py:113
  141.8 31.1 %all_gather.70 = bf16[192,768]{0,1:T(8,128)(2,1)S(1)} all-gather(bf16[192,96]{0,1:T(8,128)(2,1)S(1)} %copy.186), channel_id=1, replica_groups=mesh['dp'=4,'mem'=8] {'mem'}, dimensions={1}, use_global_device_ids=true | all-gather | bytes 331776 | tf_op jit(solution)/shard_map/all_gather | solution.py:114
  174.0 31.0 %all_gather.72 = bf16[192,768]{0,1:T(8,128)(2,1)S(1)} all-gather(bf16[192,96]{0,1:T(8,128)(2,1)S(1)} %copy.188), channel_id=1, replica_groups=mesh['dp'=4,'mem'=8] {'mem'}, dimensions={1}, use_global_device_ids=true | all-gather | bytes 331776 | tf_op jit(solution)/shard_map/all_gather | solution.py:115
  206.0 32.8 %all_gather.68 = bf16[192,768]{0,1:T(8,128)(2,1)S(1)} all-gather(bf16[192,96]{0,1:T(8,128)(2,1)S(1)} %copy.182), channel_id=1, replica_groups=mesh['dp'=4,'mem'=8] {'mem'}, dimensions={1}, use_global_device_ids=true | all-gather | bytes 331776 | tf_op jit(solution)/shard_map/all_gather | solution.py:116
  239.9 31.3 %all_gather.74 = bf16[192,768]{0,1:T(8,128)(2,1)S(1)} all-gather(bf16[192,96]{0,1:T(8,128)(2,1)S(1)} %copy.193), channel_id=1, replica_groups=mesh['dp'=4,'mem'=8] {'mem'}, dimensions={1}, use_global_device_ids=true | all-gather | bytes 331776 | tf_op jit(solution)/shard_map/all_gather | solution.py:117
  274.6 4.4 all-to-all-start
  305.9 3.5 convolution_convert_fusion.8
  314.8 3.8 convolution_convert_fusion.4
  321.1 3.8 convolution_convert_fusion.5
  327.4 3.3 multiply_reduce_fusion.2
  333.3 3.6 convolution_convert_fusion.2
  336.9 3.6 fusion.98
  342.1 8.2 fusion.13
  350.2 17.4 %all-gather.35.cloned.1.call-done = bf16[3072,768]{1,0:T(8,128)(2,1)} async-done(((bf16[768,768]{1,0:T(8,128)(2,1)}), bf16[3072,768]{1,0:T(8,128)(2,1)}) %all-gather.35.cloned.1.call-update) | async-done | bytes 4718608 | tf_op jit(solution)/shard_map/all_gather | solution.py:131
  367.6 9.0 fusion.6
  376.6 3.5 multiply_reduce_fusion.3
  390.9 5.6 multiply_reduce_fusion.1
  402.3 3.9 convert_element_type.271
  406.2 3.6 bitcast_convert_fusion.5
  409.9 3.7 fusion.93
  419.2 3.6 convolution_convert_fusion.6
  450.0 3.6 bitcast_convert_fusion.8
  466.8 8.1 bitcast_convert_fusion
  476.4 6.6 bitcast_convert_fusion.1
  489.1 6.5 reduce-scatter.45.cloned.1.call-done
  497.6 26.2 %reduce-scatter.41.cloned.1.call-done = bf16[192,768]{1,0:T(8,128)(2,1)} async-done(((bf16[768,768]{1,0:T(8,128)(2,1)}), bf16[192,768]{1,0:T(8,128)(2,1)}) %reduce-scatter.41.cloned.1.call-update) | async-done | bytes 294928 | tf_op jit(solution)/shard_map/reduce_scatter | solution.py:137
  525.7 26.4 %reduce-scatter.43.cloned.1.call-done = bf16[192,768]{1,0:T(8,128)(2,1)} async-done(((bf16[768,768]{1,0:T(8,128)(2,1)}), bf16[192,768]{1,0:T(8,128)(2,1)}) %reduce-scatter.43.cloned.1.call-update) | async-done | bytes 294928 | tf_op jit(solution)/shard_map/reduce_scatter | solution.py:140
  554.5 26.0 %reduce-scatter.73.cloned.1.call-done = bf16[192,768]{1,0:T(8,128)(2,1)} async-done(((bf16[768,768]{1,0:T(8,128)(2,1)}), bf16[192,768]{1,0:T(8,128)(2,1)}) %reduce-scatter.73.cloned.1.call-update) | async-done | bytes 294928
  582.5 26.9 %reduce-scatter.71.cloned.1.call-done = bf16[192,768]{1,0:T(8,128)(2,1)} async-done(((bf16[768,768]{1,0:T(8,128)(2,1)}), bf16[192,768]{1,0:T(8,128)(2,1)}) %reduce-scatter.71.cloned.1.call-update) | async-done | bytes 294928
  611.4 48.4 %reduce-scatter.59.cloned.1.call-done = bf16[768,768]{1,0:T(8,128)(2,1)} async-done(((bf16[3072,768]{1,0:T(8,128)(2,1)}), bf16[768,768]{1,0:T(8,128)(2,1)}) %reduce-scatter.59.cloned.1.call-update) | async-done | bytes 1179664 | tf_op jit(solution)/shard_map/reduce_scatter | solution.py:164
  667.2 5.6 all-to-all-start.1
  672.9 3.5 fusion.60
  679.0 31.4 %reduce-scatter.57.cloned.1.call-done = bf16[192,3072]{1,0:T(8,128)(2,1)} async-done(((bf16[768,3072]{1,0:T(8,128)(2,1)}), bf16[192,3072]{1,0:T(8,128)(2,1)}) %reduce-scatter.57.cloned.1.call-update) | async-done | bytes 1179664 | tf_op jit(solution)/shard_map/reduce_scatter | solution.py:161
  713.0 4.1 fusion.94
  718.5 40.6 %all-reduce = (f32[768]{0:T(1024)}, f32[768]{0:T(1024)}, f32[768]{0:T(1024)}, f32[768]{0:T(1024)}, f32[768]{0:T(1024)}, /*index=5*/f32[768]{0:T(1024)}) all-reduce(f32[768]{0:T(1024)} %get-tuple-element.99, f32[768]{0:T(1024)} %get-tuple-element.104, f32[768]{0:T(1024)} %get-tuple-element.95, ...), channel_id=1, replica_groups=mesh['dp'=4,'mem'=8] {'dp','mem'}, use_global_device_ids=true, to_apply=%region_39.40 | all-reduce | flops 4608 | bytes 36864 | tf_op jit(solution)/shard_map/psum | solution.py:316
  762.8 8.8 select_convert_fusion
  776.7 62.0 %reduce-scatter.69.cloned.1.call-done = bf16[96,192]{1,0:T(8,128)(2,1)} async-done(((bf16[768,192]{1,0:T(8,128)(2,1)}), bf16[96,192]{1,0:T(8,128)(2,1)}) %reduce-scatter.69.cloned.1.call-update) | async-done | bytes 36880
  840.3 62.2 %reduce-scatter.67.cloned.1.call-done = bf16[96,192]{1,0:T(8,128)(2,1)} async-done(((bf16[768,192]{1,0:T(8,128)(2,1)}), bf16[96,192]{1,0:T(8,128)(2,1)}) %reduce-scatter.67.cloned.1.call-update) | async-done | bytes 36880
  904.0 62.0 %reduce-scatter.65.cloned.1.call-done = bf16[96,192]{1,0:T(8,128)(2,1)} async-done(((bf16[768,192]{1,0:T(8,128)(2,1)}), bf16[96,192]{1,0:T(8,128)(2,1)}) %reduce-scatter.65.cloned.1.call-update) | async-done | bytes 36880
  967.6 62.0 %reduce-scatter.61.cloned.1.call-done = bf16[96,192]{1,0:T(8,128)(2,1)} async-done(((bf16[768,192]{1,0:T(8,128)(2,1)}), bf16[96,192]{1,0:T(8,128)(2,1)}) %reduce-scatter.61.cloned.1.call-update) | async-done | bytes 36880
  1031.1 62.1 %reduce-scatter.63.cloned.1.call-done = bf16[96,192]{1,0:T(8,128)(2,1)} async-done(((bf16[768,192]{1,0:T(8,128)(2,1)}), bf16[96,192]{1,0:T(8,128)(2,1)}) %reduce-scatter.63.cloned.1.call-update) | async-done | bytes 36880
  1094.8 62.1 %reduce-scatter.53.cloned.1.call-done = bf16[192,96]{0,1:T(8,128)(2,1)} async-done(((bf16[192,768]{0,1:T(8,128)(2,1)}), bf16[192,96]{0,1:T(8,128)(2,1)}) %reduce-scatter.53.cloned.1.call-update) | async-done | bytes 36880 | tf_op jit(solution)/shard_map/reduce_scatter | solution.py:187
  1158.5 62.0 %reduce-scatter.51.cloned.1.call-done = bf16[192,96]{0,1:T(8,128)(2,1)} async-done(((bf16[192,768]{0,1:T(8,128)(2,1)}), bf16[192,96]{0,1:T(8,128)(2,1)}) %reduce-scatter.51.cloned.1.call-update) | async-done | bytes 36880 | tf_op jit(solution)/shard_map/reduce_scatter | solution.py:184
  1222.0 64.8 %reduce-scatter.79.cloned.1.call-done = bf16[96,768]{1,0:T(8,128)(2,1)} async-done(((bf16[768,768]{1,0:T(8,128)(2,1)}), bf16[96,768]{1,0:T(8,128)(2,1)}) %reduce-scatter.79.cloned.1.call-update) | async-done | bytes 147472
  1288.7 65.4 %reduce-scatter.77.cloned.1.call-done = bf16[384,192]{1,0:T(8,128)(2,1)} async-done(((bf16[3072,192]{1,0:T(8,128)(2,1)}), bf16[384,192]{1,0:T(8,128)(2,1)}) %reduce-scatter.77.cloned.1.call-update) | async-done | bytes 147472
  (327 shorter events, 171.1 us)
Async XLA Ops:
  7.2 36.7 %copy-start.42 = (bf16[192,96]{1,0:T(8,128)(2,1)S(1)}, bf16[192,96]{1,0:T(8,128)(2,1)}, u32[]{:S(2)}) copy-start(bf16[192,96]{1,0:T(8,128)(2,1)} %param.25) | copy-start | bytes 110596
  7.2 264.9 %all-gather.29.cloned.1.call-start = ((), (), s32[]{:S(2)}) async-start(), calls=%async_computation.30 | async-start | bytes 1327104 | tf_op jit(solution)/shard_map/all_gather | solution.py:118
  7.9 68.9 %copy-start.43 = (bf16[192,96]{1,0:T(8,128)(2,1)S(1)}, bf16[192,96]{1,0:T(8,128)(2,1)}, u32[]{:S(2)}) copy-start(bf16[192,96]{1,0:T(8,128)(2,1)} %param.26) | copy-start | bytes 110596
  7.9 272.0 %all-gather.33.cloned.1.call-start = ((), (), s32[]{:S(2)}) async-start(), calls=%async_computation.32 | async-start | bytes 1327104 | tf_op jit(solution)/shard_map/all_gather | solution.py:119
  8.7 273.8 %all-gather.15.cloned.1.call-start = ((), (), s32[]{:S(2)}) async-start(), calls=%async_computation.23 | async-start | bytes 1474560 | tf_op jit(solution)/shard_map/all_gather | solution.py:122
  43.9 65.7 %copy-start.44 = (bf16[192,96]{1,0:T(8,128)(2,1)S(1)}, bf16[192,96]{1,0:T(8,128)(2,1)}, u32[]{:S(2)}) copy-start(bf16[192,96]{1,0:T(8,128)(2,1)} %param.27) | copy-start | bytes 110596
  43.9 242.6 %all-gather.17.cloned.1.call-start = ((), (), s32[]{:S(2)}) async-start(), calls=%async_computation.24 | async-start | bytes 1474560 | tf_op jit(solution)/shard_map/all_gather | solution.py:123
  76.8 65.0 %copy-start.45 = (bf16[192,96]{1,0:T(8,128)(2,1)S(1)}, bf16[192,96]{1,0:T(8,128)(2,1)}, u32[]{:S(2)}) copy-start(bf16[192,96]{1,0:T(8,128)(2,1)} %param.28) | copy-start | bytes 110596
  76.8 213.4 %all-gather.13.cloned.1.call-start = ((), (), s32[]{:S(2)}) async-start(), calls=%async_computation.22 | async-start | bytes 1474560 | tf_op jit(solution)/shard_map/all_gather | solution.py:124
  109.5 64.3 %copy-start.46 = (bf16[192,96]{1,0:T(8,128)(2,1)S(1)}, bf16[192,96]{1,0:T(8,128)(2,1)}, u32[]{:S(2)}) copy-start(bf16[192,96]{1,0:T(8,128)(2,1)} %param.29) | copy-start | bytes 110596
  109.5 191.9 %all-gather.19.cloned.1.call-start = ((), (), s32[]{:S(2)}) async-start(), calls=%async_computation.25 | async-start | bytes 1474560 | tf_op jit(solution)/shard_map/all_gather | solution.py:125
  141.7 64.2 %copy-start.47 = (bf16[192,96]{1,0:T(8,128)(2,1)S(1)}, bf16[192,96]{1,0:T(8,128)(2,1)}, u32[]{:S(2)}) copy-start(bf16[192,96]{1,0:T(8,128)(2,1)} %param.30) | copy-start | bytes 110596
  141.7 164.2 %all-gather.23.cloned.1.call-start = ((), (), s32[]{:S(2)}) async-start(), calls=%async_computation.27 | async-start | bytes 1474560 | tf_op jit(solution)/shard_map/all_gather | solution.py:126
  173.8 66.0 %copy-start.48 = (bf16[192,96]{1,0:T(8,128)(2,1)S(1)}, bf16[192,96]{1,0:T(8,128)(2,1)}, u32[]{:S(2)}) copy-start(bf16[192,96]{1,0:T(8,128)(2,1)} %param.31) | copy-start | bytes 110596
  173.8 141.0 %all-gather.25.cloned.1.call-start = ((), (), s32[]{:S(2)}) async-start(), calls=%async_computation.28 | async-start | bytes 1474560 | tf_op jit(solution)/shard_map/all_gather | solution.py:127
  205.8 115.3 %all-gather.21.cloned.1.call-start = ((), (), s32[]{:S(2)}) async-start(), calls=%async_computation.26 | async-start | bytes 1474560 | tf_op jit(solution)/shard_map/all_gather | solution.py:128
  239.7 33.1 %copy-start.36 = (bf16[64,12,768]{2,0,1:T(8,128)(2,1)S(1)}, bf16[64,12,768]{2,0,1:T(8,128)(2,1)}, u32[]{:S(2)}) copy-start(bf16[64,12,768]{2,0,1:T(8,128)(2,1)} %param.22) | copy-start | bytes 3538948
  239.7 97.2 %all-gather.27.cloned.1.call-start = ((), (), s32[]{:S(2)}) async-start(), calls=%async_computation.29 | async-start | bytes 1474560 | tf_op jit(solution)/shard_map/all_gather | solution.py:129
  272.1 70.0 %all-gather.31.cloned.1.call-start = ((), (), s32[]{:S(2)}) async-start(), calls=%async_computation.31 | async-start | bytes 5898240 | tf_op jit(solution)/shard_map/all_gather | solution.py:130
  274.6 37.3 %all-to-all-start = ((bf16[64,12,768]{2,1,0:T(8,128)(2,1)}), bf16[64,12,768]{2,1,0:T(8,128)(2,1)}, u32[]{:S(2)}, u32[]{:S(2)}) async-start(bf16[64,12,768]{2,1,0:T(8,128)(2,1)} %copy.179), calls=%async_computation | async-start | bytes 3145728 | tf_op jit(solution)/shard_map/all_to_all | solution.py:248
  279.1 88.6 %all-gather.35.cloned.1.call-start = ((), (), s32[]{:S(2)}) async-start(), calls=%async_computation.33 | async-start | bytes 5898240 | tf_op jit(solution)/shard_map/all_gather | solution.py:131
  279.8 187.0 %copy-start.53 = (pred[8,64]{1,0:T(8,128)(4,1)}, pred[8,64]{1,0:T(8,128)(4,1)S(1)}, u32[]{:S(2)}) copy-start(pred[8,64]{1,0:T(8,128)(4,1)S(1)} %iota_compare_fusion.1) | copy-start | bytes 1540
  282.4 200.7 %reduce-scatter.55.cloned.1.call-start = ((), (), s32[]{:S(2)}) async-start(), calls=%async_computation.41 | async-start | bytes 1474560 | tf_op jit(solution)/shard_map/reduce_scatter | solution.py:158
  367.6 9.0 copy-start.10
  367.6 9.0 copy-start.56
  384.8 100.4 %reduce-scatter.49.cloned.1.call-start = ((), (), s32[]{:S(2)}) async-start(), calls=%async_computation.38 | async-start | bytes 1474560 | tf_op jit(solution)/shard_map/reduce_scatter | solution.py:149
  409.8 77.3 %reduce-scatter.47.cloned.1.call-start = ((), (), s32[]{:S(2)}) async-start(), calls=%async_computation.37 | async-start | bytes 1474560 | tf_op jit(solution)/shard_map/reduce_scatter | solution.py:146
  419.2 76.5 %reduce-scatter.45.cloned.1.call-start = ((), (), s32[]{:S(2)}) async-start(), calls=%async_computation.36 | async-start | bytes 1474560 | tf_op jit(solution)/shard_map/reduce_scatter | solution.py:143
  432.0 91.8 %reduce-scatter.41.cloned.1.call-start = ((), (), s32[]{:S(2)}) async-start(), calls=%async_computation.34 | async-start | bytes 1474560 | tf_op jit(solution)/shard_map/reduce_scatter | solution.py:137
  444.2 107.9 %reduce-scatter.43.cloned.1.call-start = ((), (), s32[]{:S(2)}) async-start(), calls=%async_computation.35 | async-start | bytes 1474560 | tf_op jit(solution)/shard_map/reduce_scatter | solution.py:140
  453.6 126.9 %reduce-scatter.73.cloned.1.call-start = ((), (), s32[]{:S(2)}) async-start(), calls=%async_computation.50 | async-start | bytes 1474560
  462.3 147.1 %reduce-scatter.71.cloned.1.call-start = ((), (), s32[]{:S(2)}) async-start(), calls=%async_computation.49 | async-start | bytes 1474560
  466.7 193.0 %reduce-scatter.59.cloned.1.call-start = ((), (), s32[]{:S(2)}) async-start(), calls=%async_computation.43 | async-start | bytes 5898240 | tf_op jit(solution)/shard_map/reduce_scatter | solution.py:164
  475.0 235.4 %reduce-scatter.57.cloned.1.call-start = ((), (), s32[]{:S(2)}) async-start(), calls=%async_computation.42 | async-start | bytes 5898240 | tf_op jit(solution)/shard_map/reduce_scatter | solution.py:161
  483.0 292.1 %reduce-scatter.75.cloned.1.call-start = ((), (), s32[]{:S(2)}) async-start(), calls=%async_computation.51 | async-start | bytes 442368
  485.1 353.6 %reduce-scatter.69.cloned.1.call-start = ((), (), s32[]{:S(2)}) async-start(), calls=%async_computation.48 | async-start | bytes 442368
  487.1 415.4 %reduce-scatter.67.cloned.1.call-start = ((), (), s32[]{:S(2)}) async-start(), calls=%async_computation.47 | async-start | bytes 442368
  489.1 476.9 %reduce-scatter.65.cloned.1.call-start = ((), (), s32[]{:S(2)}) async-start(), calls=%async_computation.46 | async-start | bytes 442368
  497.5 532.0 %reduce-scatter.61.cloned.1.call-start = ((), (), s32[]{:S(2)}) async-start(), calls=%async_computation.44 | async-start | bytes 442368
  525.7 567.5 %reduce-scatter.63.cloned.1.call-start = ((), (), s32[]{:S(2)}) async-start(), calls=%async_computation.45 | async-start | bytes 442368
  554.1 602.9 %reduce-scatter.53.cloned.1.call-start = ((), (), s32[]{:S(2)}) async-start(), calls=%async_computation.40 | async-start | bytes 442368 | tf_op jit(solution)/shard_map/reduce_scatter | solution.py:187
  582.4 638.0 %reduce-scatter.51.cloned.1.call-start = ((), (), s32[]{:S(2)}) async-start(), calls=%async_computation.39 | async-start | bytes 442368 | tf_op jit(solution)/shard_map/reduce_scatter | solution.py:184
  611.3 50.9 %copy-start.33 = (bf16[8,12,64,96]{3,2,1,0:T(8,128)(2,1)S(1)}, bf16[8,12,64,96]{3,2,1,0:T(8,128)(2,1)}, u32[]{:S(2)}) copy-start(bf16[8,12,64,96]{3,2,1,0:T(8,128)(2,1)} %copy-done.32) | copy-start | bytes 3538948
  611.3 50.9 %copy-start.57 = (bf16[768,768]{1,0:T(8,128)(2,1)S(1)}, bf16[768,768]{1,0:T(8,128)(2,1)}, u32[]{:S(2)}) copy-start(bf16[768,768]{1,0:T(8,128)(2,1)} %all-gather.25.cloned.1.call-done) | copy-start | bytes 3538948
  611.3 675.4 %reduce-scatter.79.cloned.1.call-start = ((), (), s32[]{:S(2)}) async-start(), calls=%async_computation.53 | async-start | bytes 1327104
  667.2 104.4 %all-to-all-start.1 = ((bf16[8,96,768]{2,0,1:T(8,128)(2,1)}), bf16[8,96,768]{2,0,1:T(8,128)(2,1)S(1)}, u32[]{:S(2)}, u32[]{:S(2)}) async-start(bf16[8,96,768]{2,0,1:T(8,128)(2,1)} %copy.217), calls=%async_computation.1 | async-start | bytes 2359296 | tf_op jit(solution)/shard_map/all_to_all | solution.py:283
  672.8 681.3 %reduce-scatter.77.cloned.1.call-start = ((), (), s32[]{:S(2)}) async-start(), calls=%async_computation.52 | async-start | bytes 1769472
  679.0 33.9 %copy-start.8 = (bf16[8,64,768]{2,1,0:T(8,128)(2,1)S(1)}, bf16[8,64,768]{2,1,0:T(8,128)(2,1)}, u32[]{:S(2)}) copy-start(bf16[8,64,768]{2,1,0:T(8,128)(2,1)} %param.20) | copy-start | bytes 2359300
  (50 other events, 113.5 us)
Sparse Core Ops, SparseCore 0:
  10.1 46.3 all-gather.28
  58.6 42.2 all-gather.32
  103.0 16.0 all-gather.14
  121.1 17.4 all-gather.16
  140.6 17.4 all-gather.12
  160.1 17.4 all-gather.18
  179.7 17.4 all-gather.22
  206.0 18.4 all-gather.24
  239.8 17.3 all-gather.20
  272.2 17.4 all-gather.26
  291.2 37.4 all-gather.30
  330.1 37.4 all-gather.34
  384.9 25.7 reduce-scatter.54
  413.3 25.7 reduce-scatter.48
  441.5 25.7 reduce-scatter.46
  469.8 25.7 reduce-scatter.44
  498.0 25.7 reduce-scatter.40
  526.4 25.7 reduce-scatter.42
  554.7 25.7 reduce-scatter.72
  583.6 25.7 reduce-scatter.70
  611.9 47.8 reduce-scatter.58
  662.5 47.8 reduce-scatter.56
  713.6 61.4 reduce-scatter.74
  778.2 60.4 reduce-scatter.68
  842.0 60.4 reduce-scatter.66
  905.6 60.3 reduce-scatter.64
  969.1 60.3 reduce-scatter.60
  1032.8 60.3 reduce-scatter.62
  1096.5 60.3 reduce-scatter.52
  1160.0 60.3 reduce-scatter.50
  1223.8 62.9 reduce-scatter.78
  1290.2 63.8 reduce-scatter.76
where the time goes:
time: 1370 us; the launch traced here: 1360 us
  waiting for transfers between devices  779 us (57%)
  blocking collectives  295 us (22%)
  matrix products  143 us (10%)
  local copies, waits for them, and re-layouts  98.5 us (7%)
  other arithmetic  20.1 us (1%)
  between operations  15.5 us (1%)
    unnamed x42, waiting for transfers between devices  498 us
    reduce_scatter x1, waiting for transfers between devices, reduce_all(): lax.psum_scatter(row_sums[6].astype(jnp.bfloat16), 'mem', scatter_dimensi...  62.1 us
    reduce_scatter x1, waiting for transfers between devices, reduce_all(): lax.psum_scatter(row_sums[5].astype(jnp.bfloat16), 'mem', scatter_dimensi...  62 us
    unnamed x160, local copies, waits for them, and re-layouts  51.9 us
    reduce_scatter x1, waiting for transfers between devices, reduce_all(): lax.psum_scatter(grads[9].astype(jnp.bfloat16), 'dp', scatter_dimension=0...  48.4 us
    dot_general x10, matrix products, apply_mat(): jnp.einsum('bsd,de->bse', acts, matrix, preferred_element_type=jnp.float32)  41.2 us
    psum x1, blocking collectives, shards(): lax.psum((first_gain_grad, first_shift_grad, second_gain_grad, second_shi...  40.6 us
    dot_general x10, matrix products, apply_back(): jnp.einsum('bse,de->bsd', grads, matrix, preferred_element_type=jnp.float32)  36.3 us
  transfers between devices with their start and end apart: 34, of which 18 were waited for; matrix products, arithmetic and copies ran while one was open for 17% of the time, Pallas kernels for 0%

commit v1 on v0

--- a/solution.py
+++ b/solution.py
@@ -1,10 +1,17 @@
+import functools
+
 import jax
 import jax.numpy as jnp
 from jax import lax
+from jax.experimental import pallas as pl
+from jax.experimental.pallas import tpu as pltpu
 from jax.sharding import PartitionSpec as P
 
 HEADS = 12
 HEAD = 64
+MESH = pl.DeviceIdType.MESH
+BF = jnp.bfloat16
+F32 = jnp.float32
 
 
 EPS = 1e-06
@@ -196,6 +203,631 @@
         lax.psum_scatter(
             row_sums[9].astype(jnp.bfloat16), "mem", scatter_dimension=1, tiled=True
         ).astype(jnp.float32),
+    )
+
+
+class Place:
+    def __init__(self):
+        self.d = lax.axis_index("dp")
+        self.m = lax.axis_index("mem")
+        self.c = lax.rem(self.d, 2)
+        self.x = lax.div(self.d, 2)
+        self.y = lax.rem(self.m, 2)
+        self.z = lax.div(self.m, 2)
+        self.oc, self.ox, self.oy = 1 - self.c, 1 - self.x, 1 - self.y
+        self.sib = (self.x * 2 + self.oc, self.m)
+        self.xn = (self.ox * 2 + self.c, self.m)
+        self.yn = (self.d, self.z * 2 + self.oy)
+
+    def zup(self, k):
+        return lax.rem(self.z + k, 4)
+
+    def zpeer(self, k):
+        return (self.d, self.zup(k) * 2 + self.y)
+
+    def mpeer(self, k):
+        return (self.d, lax.rem(self.m + k, 8))
+
+
+def greet(at):
+    barrier = pltpu.get_barrier_semaphore()
+    for peer in [at.sib, at.xn] + [at.mpeer(k) for k in range(1, 8)]:
+        pl.semaphore_signal(barrier, inc=1, device_id=peer, device_id_type=MESH)
+    pl.semaphore_wait(barrier, 9)
+
+
+def remote(src, dst, sends, recvs, idx, peer):
+    return pltpu.make_async_remote_copy(
+        src_ref=src,
+        dst_ref=dst,
+        send_sem=sends.at[idx],
+        recv_sem=recvs.at[idx],
+        device_id=peer,
+        device_id_type=MESH,
+    )
+
+
+class Gather:
+    def __init__(self, at, full, span, stage, sends, recvs, base):
+        self.at, self.full, self.span, self.stage = at, full, span, stage
+        self.sends, self.recvs, self.base = sends, recvs, base
+        self.lanes = full.shape[-1] // 2
+        self.out = []
+
+    def piece(self, z, y, h, x):
+        lo = pl.multiple_of(x * self.lanes, 128)
+        return self.full.at[self.span, z, y, h, :, pl.ds(lo, self.lanes)]
+
+    def copy(self, slot, src, dst, peer):
+        return remote(src, dst, self.sends, self.recvs, self.base + slot, peer)
+
+    def send(self, slot, src, dst, peer):
+        copy = self.copy(slot, src, dst, peer)
+        copy.start()
+        self.out.append(copy)
+
+    def got(self, slot, ref):
+        self.copy(slot, ref, ref, self.at.sib).wait_recv()
+
+    def begin(self):
+        at = self.at
+        own = self.piece(at.z, at.y, at.c, at.x)
+        for k in (1, 2, 3):
+            self.send(k - 1, self.stage, own, at.zpeer(k))
+        self.send(3, self.stage, own, at.xn)
+        self.send(7, self.stage, own, at.yn)
+        self.send(13, self.stage, own, at.sib)
+
+    def second(self):
+        at = self.at
+        for k in (1, 2, 3):
+            ref = self.piece(at.zup(4 - k), at.y, at.c, at.x)
+            self.got(k - 1, ref)
+            self.send(3 + k, ref, ref, at.xn)
+            self.send(7 + k, ref, ref, at.yn)
+            self.send(13 + k, ref, ref, at.sib)
+
+    def third(self):
+        at = self.at
+        for k in range(4):
+            self.got(3 + k, self.piece(at.zup(4 - k), at.y, at.c, at.ox))
+        ref = self.piece(pl.ds(0, 2), at.y, at.c, at.ox)
+        self.send(11, ref, ref, at.yn)
+        ref = self.piece(slice(None), at.y, at.c, at.ox)
+        self.send(17, ref, ref, at.sib)
+        for k in range(4):
+            self.got(7 + k, self.piece(at.zup(4 - k), at.oy, at.c, at.x))
+        ref = self.piece(pl.ds(2, 2), at.oy, at.c, at.x)
+        self.send(12, ref, ref, at.xn)
+        ref = self.piece(slice(None), at.oy, at.c, at.x)
+        self.send(18, ref, ref, at.sib)
+
+    def fourth(self):
+        at = self.at
+        for half in range(2):
+            ref = self.piece(pl.ds(2 * half, 2), at.oy, at.c, at.ox)
+            self.got(11 + half, ref)
+            self.send(19 + half, ref, ref, at.sib)
+
+    def last(self):
+        at = self.at
+        for k in range(4):
+            self.got(13 + k, self.piece(at.zup(4 - k), at.y, at.oc, at.x))
+        self.got(17, self.piece(slice(None), at.y, at.oc, at.ox))
+        self.got(18, self.piece(slice(None), at.oy, at.oc, at.x))
+        for half in range(2):
+            self.got(19 + half, self.piece(pl.ds(2 * half, 2), at.oy, at.oc, at.ox))
+
+    def drain(self):
+        for copy in self.out:
+            copy.wait_send()
+        self.out = []
+
+
+GATHER_SLOTS = 21
+
+
+class Reduce:
+    def __init__(self, at, full, span, bufs, sends, recvs, base):
+        self.at, self.full, self.span = at, full, span
+        self.chip, self.rdiag, self.rx, self.ry, self.rz, self.fin = bufs
+        self.sends, self.recvs, self.base = sends, recvs, base
+        self.lanes = full.shape[-1] // 2
+        self.count = self.chip.shape[0]
+        self.out = []
+
+    send, got, copy, drain = Gather.send, Gather.got, Gather.copy, Gather.drain
+
+    def begin(self):
+        at = self.at
+        for x in range(2):
+            src = self.full.at[
+                self.span, :, :, at.oc, :, x * self.lanes : (x + 1) * self.lanes
+            ]
+            self.send(x, src, self.chip.at[:, x], at.sib)
+
+    def second(self):
+        at = self.at
+        chip, full, lanes, w0 = self.chip, self.full, self.lanes, self.span.start
+        for x in range(2):
+            self.got(x, chip.at[:, x])
+
+        def add(i, carry):
+            w, r = lax.div(i, 8), lax.rem(i, 8)
+            z, y = lax.div(r, 2), lax.rem(r, 2)
+            for x in range(2):
+                mine = full[w0 + w, z, y, at.c, :, x * lanes : (x + 1) * lanes]
+                chip[w, x, z, y] = (
+                    chip[w, x, z, y].astype(F32) + mine.astype(F32)
+                ).astype(BF)
+            return carry
+
+        lax.fori_loop(0, 8 * self.count, add, 0)
+        self.send(2, chip.at[:, at.ox, pl.ds(0, 2), at.oy], self.rdiag.at[0], at.yn)
+        self.send(3, chip.at[:, at.ox, pl.ds(2, 2), at.oy], self.rdiag.at[1], at.xn)
+
+    def third(self):
+        at, chip = self.at, self.chip
+        for half in range(2):
+            self.got(2 + half, self.rdiag.at[half])
+            x, y = ((at.ox, at.y), (at.x, at.oy))[half]
+
+            def add(i, carry, x=x, y=y, half=half):
+                w, z = lax.div(i, 2), lax.rem(i, 2)
+                chip[w, x, 2 * half + z, y] = (
+                    chip[w, x, 2 * half + z, y].astype(F32)
+                    + self.rdiag[half, w, z].astype(F32)
+                ).astype(BF)
+                return carry
+
+            lax.fori_loop(0, 2 * self.count, add, 0)
+        self.send(4, chip.at[:, at.ox, :, at.y], self.rx, at.xn)
+        self.send(5, chip.at[:, at.x, :, at.oy], self.ry, at.yn)
+
+    def fourth(self):
+        at, chip = self.at, self.chip
+        self.got(4, self.rx)
+        self.got(5, self.ry)
+
+        def add(i, carry):
+            w, z = lax.div(i, 4), lax.rem(i, 4)
+            chip[w, at.x, z, at.y] = (
+                chip[w, at.x, z, at.y].astype(F32)
+                + self.rx[w, z].astype(F32)
+                + self.ry[w, z].astype(F32)
+            ).astype(BF)
+            return carry
+
+        lax.fori_loop(0, 4 * self.count, add, 0)
+        for k in (1, 2, 3):
+            self.send(
+                5 + k, chip.at[:, at.x, at.zup(k), at.y], self.rz.at[k - 1], at.zpeer(k)
+            )
+
+    def fifth(self):
+        at = self.at
+        for k in (1, 2, 3):
+            self.got(5 + k, self.rz.at[k - 1])
+
+        def add(w, carry):
+            total = self.chip[w, at.x, at.z, at.y].astype(F32)
+            for k in range(3):
+                total = total + self.rz[k, w].astype(F32)
+            self.fin[at.c, w] = total.astype(BF)
+            return carry
+
+        lax.fori_loop(0, self.count, add, 0)
+        self.send(9, self.fin.at[at.c], self.fin.at[at.c], at.sib)
+
+    def last(self):
+        self.got(9, self.fin.at[self.at.oc])
+
+
+REDUCE_SLOTS = 10
+
+
+def reduce_bufs(count, rows, lanes):
+    return [
+        pltpu.VMEM((count, 2, 4, 2, rows, lanes), BF),
+        pltpu.VMEM((2, count, 2, rows, lanes), BF),
+        pltpu.VMEM((count, 4, rows, lanes), BF),
+        pltpu.VMEM((count, 4, rows, lanes), BF),
+        pltpu.VMEM((3, count, rows, lanes), BF),
+        pltpu.VMEM((2, count, rows, lanes), BF),
+    ]
+
+
+def pick(rows, cols, start):
+    col = lax.broadcasted_iota(jnp.int32, (rows, cols), 1)
+    row = lax.broadcasted_iota(jnp.int32, (rows, cols), 0)
+    return jnp.where(col == row + start, 1.0, 0.0).astype(BF)
+
+
+def dot_nt(a, b):
+    return lax.dot_general(a, b, (((1,), (1,)), ((), ())), preferred_element_type=F32)
+
+
+def gather_kernel(*refs):
+    shards, rows = refs[:10], refs[10]
+    out_s, out_in, out_out, out_rows = refs[11:15]
+    (full_s, full_in, full_out, pair_s, pair_in, pair_out, stage_s, stage_in, stage_out,
+     psend, precv, gsend, grecv, rsend, rrecv, local) = refs[15:]
+    at = Place()
+    greet(at)
+    pairs = [pair_s.at[i] for i in range(8)] + [pair_in, pair_out]
+    own, other = [], []
+    for i in range(10):
+        depth = shards[i].shape[0]
+        mine = pairs[i].at[pl.ds(pl.multiple_of(at.c * depth, 8), depth), :]
+        copy = remote(shards[i], mine, psend, precv, i, at.sib)
+        copy.start()
+        other.append(copy)
+        copy = pltpu.make_async_copy(shards[i], mine, local.at[i])
+        copy.start()
+        own.append(copy)
+
+    def ready(i):
+        own[i].wait()
+        depth = shards[i].shape[0]
+        theirs = pairs[i].at[pl.ds(pl.multiple_of(at.oc * depth, 8), depth), :]
+        remote(theirs, theirs, psend, precv, i, at.sib).wait_recv()
+
+    groups = [
+        Gather(at, full_s, slice(0, 3), stage_s.at[0:3], gsend, grecv, 0),
+        Gather(at, full_s, slice(3, 8), stage_s.at[3:8], gsend, grecv, GATHER_SLOTS),
+        Gather(at, full_in, slice(0, 1), stage_in, gsend, grecv, 2 * GATHER_SLOTS),
+        Gather(at, full_out, slice(0, 1), stage_out, gsend, grecv, 3 * GATHER_SLOTS),
+    ]
+    locals_ = []
+    for g, group in enumerate(groups):
+        if g < 2:
+            half = stage_s.shape[1]
+            sel = pick(half, 2 * half, at.c * half)
+            for i in range(group.span.start, group.span.stop):
+                ready(i)
+                stage_s[i] = dot_nt(sel, pair_s[i]).astype(BF)
+        else:
+            ready(6 + g)
+            stage, pair = ((stage_in, pair_in), (stage_out, pair_out))[g - 2]
+            half = stage.shape[1]
+            stage[0] = dot_nt(pick(half, 2 * half, at.c * half), pair[...]).astype(BF)
+        group.begin()
+        copy = pltpu.make_async_copy(
+            group.stage, group.piece(at.z, at.y, at.c, at.x), local.at[10 + g]
+        )
+        copy.start()
+        locals_.append(copy)
+    mems = []
+    for k in range(1, 8):
+        to = lax.rem(at.m + k, 8)
+        copy = remote(rows.at[to], out_rows.at[at.m], rsend, rrecv, k - 1, at.mpeer(k))
+        copy.start()
+        mems.append(copy)
+    copy = pltpu.make_async_copy(rows.at[at.m], out_rows.at[at.m], local.at[14])
+    copy.start()
+    locals_.append(copy)
+    for group in groups:
+        group.second()
+    for group in groups:
+        group.third()
+    for group in groups:
+        group.fourth()
+    for group in groups:
+        group.last()
+    for k in range(1, 8):
+        ref = out_rows.at[lax.rem(at.m + 8 - k, 8)]
+        remote(ref, ref, rsend, rrecv, k - 1, at.sib).wait_recv()
+    for copy in locals_:
+        copy.wait()
+    ends = []
+    for i, (a, b) in enumerate(
+        ((full_s, out_s), (full_in, out_in), (full_out, out_out))
+    ):
+        copy = pltpu.make_async_copy(a, b, local.at[i])
+        copy.start()
+        ends.append(copy)
+    for copy in ends:
+        copy.wait()
+    for copy in other + mems:
+        copy.wait_send()
+    for group in groups:
+        group.drain()
+
+
+def gather_all(shards, rows):
+    depth, width = shards[0].shape
+    dmodel = depth * 4
+    half = width // 2
+    half_in = shards[8].shape[1] // 2
+    ff = half_in * 16
+    shapes = [
+        (8, 4, 2, 2, half, dmodel),
+        (1, 4, 2, 2, half_in, dmodel),
+        (1, 4, 2, 2, half, ff),
+    ]
+    any_ = pl.BlockSpec(memory_space=pl.ANY)
+    return pl.pallas_call(
+        gather_kernel,
+        out_shape=[jax.ShapeDtypeStruct(s, BF) for s in shapes]
+        + [jax.ShapeDtypeStruct(rows.shape, BF)],
+        in_specs=[any_] * 11,
+        out_specs=[any_] * 4,
+        scratch_shapes=[pltpu.VMEM(s, BF) for s in shapes]
+        + [
+            pltpu.VMEM((8, 2 * depth, width), BF),
+            pltpu.VMEM((2 * depth, 2 * half_in), BF),
+            pltpu.VMEM((ff // 2, width), BF),
+            pltpu.VMEM((8, half, 2 * depth), BF),
+            pltpu.VMEM((1, half_in, 2 * depth), BF),
+            pltpu.VMEM((1, half, ff // 2), BF),
+            pltpu.SemaphoreType.DMA((10,)),
+            pltpu.SemaphoreType.DMA((10,)),
+            pltpu.SemaphoreType.DMA((4 * GATHER_SLOTS,)),
+            pltpu.SemaphoreType.DMA((4 * GATHER_SLOTS,)),
+            pltpu.SemaphoreType.DMA((7,)),
+            pltpu.SemaphoreType.DMA((7,)),
+            pltpu.SemaphoreType.DMA((15,)),
+        ],
+        compiler_params=pltpu.CompilerParams(
+            collective_id=0, has_side_effects=True, vmem_limit_bytes=60 << 20
+        ),
+    )(*shards, rows)
+
+
+def reduce_kernel(*refs):
+    in_s, in_in, in_out, rows = refs[:4]
+    outs, out_rows = refs[4:14], refs[14]
+    full_s, full_in, full_out = refs[15:18]
+    bufs = [refs[18 + 6 * g : 24 + 6 * g] for g in range(3)]
+    gsend, grecv, rsend, rrecv, local = refs[36:]
+    at = Place()
+    loads = []
+    for i, (a, b) in enumerate(((in_out, full_out), (in_in, full_in), (in_s, full_s))):
+        copy = pltpu.make_async_copy(a, b, local.at[i])
+        copy.start()
+        loads.append(copy)
+    greet(at)
+    groups = [
+        Reduce(at, full_out, slice(0, 1), bufs[0], gsend, grecv, 0),
+        Reduce(at, full_in, slice(0, 1), bufs[1], gsend, grecv, REDUCE_SLOTS),
+        Reduce(at, full_s, slice(0, 8), bufs[2], gsend, grecv, 2 * REDUCE_SLOTS),
+    ]
+    for load, group in zip(loads, groups):
+        load.wait()
+        group.begin()
+    mems = []
+    for k in range(1, 8):
+        to = lax.rem(at.m + k, 8)
+        copy = remote(rows.at[to], out_rows.at[at.m], rsend, rrecv, k - 1, at.mpeer(k))
+        copy.start()
+        mems.append(copy)
+    own = pltpu.make_async_copy(rows.at[at.m], out_rows.at[at.m], local.at[3])
+    own.start()
+    for group in groups:
+        group.second()
+    for group in groups:
+        group.third()
+    for group in groups:
+        group.fourth()
+    for group in groups:
+        group.fifth()
+    for group in groups:
+        group.last()
+    fin_out, fin_in, fin_s = (group.fin for group in groups)
+
+    def lay(out, fin, w):
+        both = jnp.concatenate([fin[0, w], fin[1, w]], axis=0)
+        depth = out.shape[0]
+        out[...] = dot_nt(pick(depth, 2 * depth, at.c * depth), both)
+
+    for w in range(8):
+        lay(outs[w], fin_s, w)
+    lay(outs[8], fin_in, 0)
+    lay(outs[9], fin_out, 0)
+    own.wait()
+    for k in range(1, 8):
+        ref = out_rows.at[lax.rem(at.m + 8 - k, 8)]
+        remote(ref, ref, rsend, rrecv, k - 1, at.sib).wait_recv()
+    for copy in mems:
+        copy.wait_send()
+    for group in groups:
+        group.drain()
+
+
+def reduce_everything(full_s, full_in, full_out, rows, shapes):
+    half, dmodel = full_s.shape[-2:]
+    half_in = full_in.shape[-2]
+    ff = full_out.shape[-1]
+    any_ = pl.BlockSpec(memory_space=pl.ANY)
+    vmem = pl.BlockSpec(memory_space=pltpu.VMEM)
+    return pl.pallas_call(
+        reduce_kernel,
+        out_shape=[jax.ShapeDtypeStruct(s, F32) for s in shapes]
+        + [jax.ShapeDtypeStruct(rows.shape, BF)],
+        in_specs=[any_] * 4,
+        out_specs=[vmem] * 10 + [any_],
+        scratch_shapes=[pltpu.VMEM(a.shape, BF) for a in (full_s, full_in, full_out)]
+        + reduce_bufs(1, half, ff // 2)
+        + reduce_bufs(1, half_in, dmodel // 2)
+        + reduce_bufs(8, half, dmodel // 2)
+        + [
+            pltpu.SemaphoreType.DMA((3 * REDUCE_SLOTS,)),
+            pltpu.SemaphoreType.DMA((3 * REDUCE_SLOTS,)),
+            pltpu.SemaphoreType.DMA((7,)),
+            pltpu.SemaphoreType.DMA((7,)),
+            pltpu.SemaphoreType.DMA((4,)),
+        ],
+        compiler_params=pltpu.CompilerParams(
+            collective_id=1, has_side_effects=True, vmem_limit_bytes=60 << 20
+        ),
+    )(full_s, full_in, full_out, rows)
+
+
+def apply_t(acts, matrix):
+    return jnp.einsum("bsd,ed->bse", acts, matrix, preferred_element_type=F32)
+
+
+def apply_back_t(grads, matrix):
+    return jnp.einsum("bse,ed->bsd", grads, matrix, preferred_element_type=F32)
+
+
+def mat_grad_t(acts, grads):
+    return jnp.einsum("bse,bsd->ed", grads, acts, preferred_element_type=F32)
+
+def shards_lean(
+    text,
+    lengths,
+    memory,
+    out_grad,
+    self_query,
+    self_key,
+    self_value,
+    self_output,
+    cross_query,
+    cross_key,
+    cross_value,
+    cross_output,
+    hidden_in,
+    hidden_out,
+    first_gain,
+    first_shift,
+    second_gain,
+    second_shift,
+    third_gain,
+    third_shift,
+):
+    mats = (
+        self_query,
+        self_key,
+        self_value,
+        self_output,
+        cross_query,
+        cross_key,
+        cross_value,
+        cross_output,
+        hidden_in,
+        hidden_out,
+    )
+    owners, length = memory.shape[0] // 8, memory.shape[1]
+    dmodel = memory.shape[2]
+    full_s, full_in, full_out, landed = gather_all(mats, memory.reshape(8, owners * length, dmodel))
+    full_mats = tuple(full_s.reshape(8, dmodel, dmodel)) + (full_in.reshape(-1, dmodel), full_out.reshape(dmodel, -1))
+    w_query, w_key, w_value, w_output, m_query, m_key, m_value, m_output, w_in, w_out = full_mats
+    places = jnp.arange(text.shape[1])
+    valid_row = places[None, :] < lengths[:, None]
+    allowed = (places[None, :] <= places[:, None])[None, None] & valid_row[:, None, None, :]
+    residual = text.astype(jnp.float32)
+    first = layer_norm(residual, first_gain, first_shift).astype(jnp.bfloat16)
+    queries = apply_t(first, w_query).astype(jnp.bfloat16)
+    keys = apply_t(first, w_key).astype(jnp.bfloat16)
+    values = apply_t(first, w_value).astype(jnp.bfloat16)
+    self_mixed, self_lse = attend_fwd(queries, keys, values, allowed)
+    after_self = residual + apply_t(self_mixed, w_output)
+    memory_rows = landed.reshape(8, owners, length, dmodel).transpose(1, 0, 2, 3).reshape(owners, 8 * length, dmodel)
+    second = layer_norm(after_self, second_gain, second_shift).astype(jnp.bfloat16)
+    cross_queries = apply_t(second, m_query).astype(jnp.bfloat16)
+    mem_keys = apply_t(memory_rows, m_key).astype(jnp.bfloat16)
+    mem_values = apply_t(memory_rows, m_value).astype(jnp.bfloat16)
+    cross_mixed, cross_lse = attend_fwd(cross_queries, mem_keys, mem_values, None)
+    after_cross = after_self + apply_t(cross_mixed, m_output)
+    third = layer_norm(after_cross, third_gain, third_shift).astype(jnp.bfloat16)
+    before_act = apply_t(third, w_in)
+    activated = jax.nn.gelu(before_act).astype(jnp.bfloat16)
+    final = after_cross + apply_t(activated, w_out)
+    layer_out = jnp.where(valid_row[:, :, None], final, 0.0).astype(jnp.bfloat16)
+    b_query, b_key, b_value, b_output, n_query, n_key, n_value, n_output, b_in, b_out = full_mats
+    grad_top = jnp.where(valid_row[:, :, None], out_grad.astype(jnp.float32), 0.0)
+    top_low = grad_top.astype(jnp.bfloat16)
+    hidden_out_grad = mat_grad_t(activated, top_low)
+    _, gelu_pull = jax.vjp(jax.nn.gelu, before_act)
+    act_low = gelu_pull(apply_back_t(top_low, b_out))[0].astype(jnp.bfloat16)
+    hidden_in_grad = mat_grad_t(third, act_low)
+    cross_input, third_gain_grad, third_shift_grad = norm_back(
+        after_cross, third_gain, third_shift, apply_back_t(act_low, b_in)
+    )
+    grad_cross = grad_top + cross_input
+    cross_low = grad_cross.astype(jnp.bfloat16)
+    cross_output_grad = mat_grad_t(cross_mixed, cross_low)
+    mixed_up = apply_back_t(cross_low, n_output).astype(jnp.bfloat16)
+    cross_query_low, mem_key_low, mem_value_low = attend_back(
+        cross_queries, mem_keys, mem_values, None, cross_lse, mixed_up
+    )
+    cross_query_grad = mat_grad_t(second, cross_query_low)
+    cross_key_grad = mat_grad_t(memory_rows, mem_key_low)
+    cross_value_grad = mat_grad_t(memory_rows, mem_value_low)
+    mem_back = (apply_back_t(mem_key_low, n_key) + apply_back_t(mem_value_low, n_value)).astype(
+        jnp.bfloat16
+    )
+    mem_back = mem_back.reshape(owners, 8, length, dmodel).transpose(1, 0, 2, 3).reshape(8, owners * length, dmodel)
+    self_input, second_gain_grad, second_shift_grad = norm_back(
+        after_self, second_gain, second_shift, apply_back_t(cross_query_low, n_query)
+    )
+    grad_self = grad_cross + self_input
+    self_low = grad_self.astype(jnp.bfloat16)
+    self_output_grad = mat_grad_t(self_mixed, self_low)
+    self_up = apply_back_t(self_low, b_output).astype(jnp.bfloat16)
+    query_low, key_low, value_low = attend_back(queries, keys, values, allowed, self_lse, self_up)
+    self_query_grad = mat_grad_t(first, query_low)
+    self_key_grad = mat_grad_t(first, key_low)
+    self_value_grad = mat_grad_t(first, value_low)
+    first_up = (
+        apply_back_t(query_low, b_query) + apply_back_t(key_low, b_key) + apply_back_t(value_low, b_value)
+    )
+    text_input, first_gain_grad, first_shift_grad = norm_back(
+        residual, first_gain, first_shift, first_up
+    )
+    text_grad = (grad_self + text_input).astype(jnp.bfloat16)
+    small = jnp.stack(
+        [
+            self_query_grad,
+            self_key_grad,
+            self_value_grad,
+            self_output_grad,
+            cross_query_grad,
+            cross_key_grad,
+            cross_value_grad,
+            cross_output_grad,
+        ]
+    ).astype(BF)
+    *weight_sums, back = reduce_everything(
+        small.reshape(full_s.shape),
+        hidden_in_grad.astype(BF).reshape(full_in.shape),
+        hidden_out_grad.astype(BF).reshape(full_out.shape),
+        mem_back,
+        [mat.shape for mat in mats],
+    )
+    memory_grad = back.reshape(memory.shape)
+    norm_sums = lax.psum(
+        (
+            first_gain_grad,
+            first_shift_grad,
+            second_gain_grad,
+            second_shift_grad,
+            third_gain_grad,
+            third_shift_grad,
+        ),
+        ("dp", "mem"),
+    )
+    return (
+        layer_out,
+        text_grad,
+        memory_grad,
+        weight_sums[0],
+        weight_sums[1],
+        weight_sums[2],
+        weight_sums[3],
+        weight_sums[4],
+        weight_sums[5],
+        weight_sums[6],
+        weight_sums[7],
+        weight_sums[8],
+        weight_sums[9],
+        norm_sums[0],
+        norm_sums[1],
+        norm_sums[2],
+        norm_sums[3],
+        norm_sums[4],
+        norm_sums[5],
     )
 
 
@@ -348,8 +980,9 @@
 
 
 def solution(mesh):
+    fits = mesh.shape["dp"] == 4 and mesh.shape["mem"] == 8
     return jax.shard_map(
-        shards,
+        shards_lean if fits else shards,
         mesh=mesh,
         in_specs=(
             P(("dp", "mem"), None, None),

time: 1370 us -> 573 us (0.42)
  waiting for transfers between devices: 779 us -> 0 us
  blocking collectives: 295 us -> 45.6 us
  Pallas kernels: 0 us -> 243 us
  local copies, waits for them, and re-layouts: 98.5 us -> 139 us
  matrix products: 143 us -> 122 us
    unnamed x42 -> x0, waiting for transfers between devices: 498 us -> none
    reduce_scatter x10 -> x0, waiting for transfers between devices: 263 us -> none  [the longest x1 62.1 us: reduce_all(): lax.psum_scatter(row_sums[6].astype(jnp.bfloat16), 'mem', scatter_dimensi...]
    all_gather x8 -> x0, blocking collectives: 254 us -> none  [the longest x1 33.3 us: fetch_weights(): lax.all_gather(mats[0], 'mem', axis=1, tiled=True)]
    pallas_call x0 -> x2, Pallas kernels: none -> 243 us  [the longest x1 124 us: reduce_everything(): pl.pallas_call(reduce_kernel, out_shape=[jax.ShapeDtypeStruct(s, F32) for...]
    another operation x0 -> x9, local copies, waits for them, and re-layouts: none -> 67.7 us
    unnamed x160 -> x193, local copies, waits for them, and re-layouts: 51.9 us -> 23.2 us
    dot_general x30, matrix products: 113 us -> 95.2 us  [the longest x10 46.8 us: mat_grad_t(): return jnp.einsum('bse,bsd->ed', grads, acts, preferred_element_type=F32)]
    all_gather x12 -> x0, waiting for transfers between devices: 17.5 us -> none  [the longest x1 17.4 us: fetch_weights(): lax.all_gather(columns[9], 'dp', axis=0, tiled=True)]
  transfers between devices with their start and end apart: 34 -> 0, of which waited for: 18 -> 0; matrix products, arithmetic and copies ran while one was open for 17% -> 0% of each run, Pallas kernels for 0% -> 0%
where the time goes in v1:
time: 573 us; the launch traced here: 565 us
  Pallas kernels  243 us (42%)
  local copies, waits for them, and re-layouts  139 us (24%)
  matrix products  122 us (21%)
  blocking collectives  45.6 us (8%)
  other arithmetic  12.6 us (2%)
    pallas_call x1, Pallas kernels, reduce_everything(): pl.pallas_call(reduce_kernel, out_shape=[jax.ShapeDtypeStruct(s, F32) for...  124 us
    pallas_call x1, Pallas kernels, gather_all(): pl.pallas_call(gather_kernel, out_shape=[jax.ShapeDtypeStruct(s, BF) for...  118 us
    another operation x8, local copies, waits for them, and re-layouts  61.1 us
    dot_general x10, matrix products, mat_grad_t(): return jnp.einsum('bse,bsd->ed', grads, acts, preferred_element_type=F32)  46.8 us
    psum x1, blocking collectives, shards_lean(): lax.psum((first_gain_grad, first_shift_grad, second_gain_grad, second_shi...  45.6 us
    dot_general x10, matrix products, apply_back_t(): return jnp.einsum('bse,ed->bsd', grads, matrix, preferred_element_type=F32)  29 us
    unnamed x193, local copies, waits for them, and re-layouts  23.2 us
    dot_general x10, matrix products, apply_t(): return jnp.einsum('bsd,ed->bse', acts, matrix, preferred_element_type=F32)  19.4 us

profile of v1, /device:TPU:0, one launch (start us, length us, event | category | flops | bytes accessed | tf_op | source)
XLA Modules:
  0.0 564.8 jit_solution(1345564095633228891)
XLA Ops:
  5.5 118.5 %shard_map.339 = (bf16[8,4,2,2,48,768]{5,4,3,2,1,0:T(8,128)(2,1)}, bf16[1,4,2,2,192,768]{5,4,3,2,1,0:T(8,128)(2,1)}, bf16[1,4,2,2,48,3072]{5,4,3,2,1,0:T(8,128)(2,1)}, bf16[8,96,768]{2,1,0:T(8,128)(2,1)}) custom-call(bf16[192,96]{1,0:T(8,128)(2,1)} %refs_0_.1, bf16[192,96]{1,0:T(8,128)(2,1)} %refs_1_.1, bf16[192,96]{1,0:T(8,128)(2,1)} %refs_2_.1, ...), custom_call_target="tpu_custom_call" | custom-call | tf_op jit(solution)/shard_map/pallas_call | solution.py:549
  124.0 6.6 %fusion.128 = (bf16[1,4,2,2,48,768]{5,4,3,2,1,0:T(8,128)(2,1)}, bf16[1,4,2,2,48,768]{5,4,3,2,1,0:T(8,128)(2,1)}, bf16[1,4,2,2,48,768]{5,4,3,2,1,0:T(8,128)(2,1)}...) fusion(bf16[8,4,2,2,48,768]{5,4,3,2,1,0:T(8,128)(2,1)} %get-tup, ...), kind=kLoop, calls=%fused_computation.163 | loop fusion | bytes 18874368 | tf_op jit(solution)/shard_map/unstack | solution.py:714
  137.0 2.8 fusion.129
  144.3 4.0 reshape.389
  148.3 2.7 convolution_convert_fusion.3
  154.8 2.2 convolution_convert_fusion.5
  157.0 2.5 copy.87
  165.4 2.5 copy.89
  167.9 3.3 multiply_reduce_fusion.2
  173.1 3.2 convolution_convert_fusion.2
  178.6 2.7 fusion.111
  181.4 4.8 select_convert_fusion
  186.3 7.9 %fusion.6 = bf16[8,64,3072]{2,1,0:T(8,128)(2,1)S(1)} fusion(f32[8,64,3072]{2,1,0:T(8,128)S(1)} %fusion.111, bf16[768,3072,1]{1,0,2:T(8,128)(2,1)S(1)} %bitcast.324, bf16[8,64,768]{2,1,0:T(8,128)(2,1)S(1)} %copy-done.42, pred[8,64]{1,0:T(8,128)(4,1)S(1)} %copy-done.74), kind=kOutput, calls=%fused_computation.10 | convolution fusion | flops 2448556032 | bytes 14942720 | tf_op jit(solution)/shard_map/bse,ed->bsd/dot_general | solution.py:671
  194.2 2.9 multiply_reduce_fusion.3
  201.5 2.6 copy.171
  204.1 4.2 multiply_reduce_fusion.1
  211.4 2.4 copy.94
  213.8 3.9 convert_element_type.201
  217.7 3.0 fusion.125
  226.8 2.7 copy.172
  229.6 3.5 convolution_convert_fusion.1
  239.8 2.4 copy.100
  242.2 3.9 convert_element_type.207
  246.1 3.6 fusion.132
  250.7 2.4 copy.104
  253.1 4.3 convert_element_type.210
  257.4 3.8 fusion.126
  264.1 8.9 %reshape.401 = bf16[4,2,2,48,8,64]{3,2,1,0,5,4:T(2,128)(2,1)} reshape(bf16[768,8,64]{0,2,1:T(8,128)(2,1)} %bitcast.309) | data formatting | bytes 1572864 | tf_op jit(solution)/shard_map/reshape.281
  273.0 4.2 fusion.63
  277.3 8.9 %reshape.402 = bf16[4,2,2,48,8,64]{3,2,1,0,5,4:T(2,128)(2,1)} reshape(bf16[768,8,64]{0,2,1:T(8,128)(2,1)} %bitcast.286) | data formatting | bytes 1572864 | tf_op jit(solution)/shard_map/reshape.283
  286.2 4.2 fusion.69
  290.3 2.4 copy.110
  292.8 9.1 %reshape.403 = bf16[4,2,2,48,8,64]{3,2,1,0,5,4:T(2,128)(2,1)} reshape(bf16[768,8,64]{0,2,1:T(8,128)(2,1)} %bitcast.310) | data formatting | bytes 1572864 | tf_op jit(solution)/shard_map/reshape.285
  301.8 4.2 fusion.75
  306.0 8.9 %reshape.404 = bf16[4,2,2,48,8,64]{3,2,1,0,5,4:T(2,128)(2,1)} reshape(bf16[768,8,64]{0,2,1:T(8,128)(2,1)} %get-tuple-element.104) | data formatting | bytes 1572864 | tf_op jit(solution)/shard_map/reshape.287
  314.9 4.9 fusion.81
  319.8 9.1 %reshape.405 = bf16[4,2,2,48,8,64]{3,2,1,0,5,4:T(2,128)(2,1)} reshape(bf16[768,8,64]{0,2,1:T(8,128)(2,1)} %bitcast.285) | data formatting | bytes 1572864 | tf_op jit(solution)/shard_map/reshape.289
  329.0 4.6 fusion.87
  335.3 4.5 copy.150
  339.8 4.7 fusion.57
  346.6 3.3 copy.153
  350.0 3.8 fusion.59
  353.7 8.4 %reshape.408 = bf16[4,2,2,48,8,64]{3,2,1,0,5,4:T(2,128)(2,1)S(1)} reshape(bf16[768,8,64]{0,2,1:T(8,128)(2,1)} %bitcast.308) | data formatting | bytes 1572864 | tf_op jit(solution)/shard_map/reshape.295
  362.1 4.5 fusion.93.refs_0_
  366.6 7.0 %bitcast_convert_fusion.1 = bf16[3072,768]{1,0:T(8,128)(2,1)} fusion(bf16[8,64,3072]{2,1,0:T(8,128)(2,1)} %copy-done.83, f32[8,64,768]{2,1,0:T(8,128)S(1)} %copy-done.15, f32[768]{0:T(1024)S(1)} %copy-done.80, f32[768]{0:T(1024)S(1)} %copy-done.77, f32[8,64]{1,0:T(8,128)S(1)} %fusion.114, f32[8,64]{1,0:T(8,128)S(1)} %broadcast_multiply_fusion), kind=kOutput, calls=%fused_computation.1 | convolution fusion | flops 2420244480 | bytes 9447424 | tf_op jit(solution)/shard_map/bse,bsd->ed/dot_general | solution.py:675
  373.6 4.9 bitcast_convert_fusion
  384.0 124.4 %shard_map.340 = (f32[192,96]{1,0:T(8,128)}, f32[192,96]{1,0:T(8,128)}, f32[192,96]{1,0:T(8,128)}, f32[192,96]{1,0:T(8,128)}, f32[192,96]{1,0:T(8,128)}, /*index...) custom-call(bf16[8,4,2,2,48,768]{5,4,3,2,1,0:T(8,128)(2,1)} %fusion., ...), custom_call_target="tpu_custom_call" | custom-call | tf_op jit(solution)/shard_map/pallas_call | solution.py:643
  512.9 45.6 %all-reduce = (f32[768]{0:T(1024)}, f32[768]{0:T(1024)}, f32[768]{0:T(1024)}, f32[768]{0:T(1024)}, f32[768]{0:T(1024)}, /*index=5*/f32[768]{0:T(1024)}) all-reduce(f32[768]{0:T(1024)S(1)} %get-tuple-element.91, f32[768]{0:T(1024)S(1)} %get-tuple-element.96, ...), channel_id=1, replica_groups=mesh['dp'=4,'mem'=8] {'dp','mem'}, use_global_device_ids=true, to_apply=%region_19.20 | all-reduce | flops 4608 | bytes 36864 | tf_op jit(solution)/shard_map/psum | solution.py:800
  (255 shorter events, 72.8 us)
Async XLA Ops:
  124.0 6.7 %copy-start.5 = (bf16[8,64,768]{2,1,0:T(8,128)(2,1)S(1)}, bf16[8,64,768]{2,1,0:T(8,128)(2,1)}, u32[]{:S(2)}) copy-start(bf16[8,64,768]{2,1,0:T(8,128)(2,1)} %param.20) | copy-start | bytes 2359300
  130.6 3.7 copy-start.33
  131.7 9.0 %copy-start.71 = (f32[8,64]{1,0:T(8,128)}, f32[8,64]{1,0:T(8,128)S(1)}, u32[]{:S(2)}) copy-start(f32[8,64]{1,0:T(8,128)S(1)} %fusion.112) | copy-start | bytes 6148
  139.8 8.5 %copy-start = (f32[8,12,64,64]{2,3,1,0:T(8,128)}, f32[8,12,64,64]{2,3,1,0:T(8,128)S(1)}, u32[]{:S(2)}) copy-start(f32[8,12,64,64]{2,3,1,0:T(8,128)S(1)} %get-tuple-element.117) | copy-start | bytes 4718596
  139.8 8.5 %copy-start.50 = (f32[8,12,64]{2,1,0:T(8,128)}, f32[8,12,64]{2,1,0:T(8,128)S(1)}, u32[]{:S(2)}) copy-start(f32[8,12,64]{2,1,0:T(8,128)S(1)} %get-tuple-element.116) | copy-start | bytes 73732
  140.7 7.6 %copy-start.54 = (f32[8,12,64]{2,1,0:T(8,128)}, f32[8,12,64]{2,1,0:T(8,128)S(1)}, u32[]{:S(2)}) copy-start(f32[8,12,64]{2,1,0:T(8,128)S(1)} %fusion.7) | copy-start | bytes 73732
  152.6 7.9 %copy-start.2 = (f32[8,64,768]{2,1,0:T(8,128)}, f32[8,64,768]{2,1,0:T(8,128)S(1)}, u32[]{:S(2)}) copy-start(f32[8,64,768]{2,1,0:T(8,128)S(1)} %get-tuple-element.119) | copy-start | bytes 4718596
  154.2 9.0 %copy-start.26 = (bf16[8,8,12,768]{3,0,2,1:T(8,128)(2,1)}, bf16[8,8,12,768]{3,0,2,1:T(8,128)(2,1)S(1)}, u32[]{:S(2)}) copy-start(bf16[8,8,12,768]{3,0,2,1:T(8,128)(2,1)S(1)} %copy.85) | copy-start | bytes 3538948
  157.0 3.5 copy-start.64
  171.2 7.0 %slice-start = ((s8[4718592]{0:T(1024)(128)(4,1)}), s8[4194304]{0:T(1024)(128)(4,1)S(1)}, s32[]{:S(2)}) async-start(s8[4718592]{0:T(1024)(128)(4,1)} %bitcast.317), calls=%async_computation | async-start | bytes 8388608
  173.1 3.2 copy-start.3
  173.1 3.2 copy-start.35
  173.1 5.1 slice-start.1
  177.8 19.3 %copy-start.14 = (f32[8,64,768]{2,1,0:T(8,128)}, f32[8,64,768]{2,1,0:T(8,128)S(1)}, u32[]{:S(2)}) copy-start(f32[8,64,768]{2,1,0:T(8,128)S(1)} %get-tuple-element.123) | copy-start | bytes 4718596
  177.9 3.5 slice-start.2
  181.4 4.9 copy-start.82
  181.4 4.9 copy-start.42
  217.7 3.1 copy-start.4
  229.6 3.5 copy-start.39
  229.6 5.6 copy-start.13
  229.6 5.6 copy-start.27
  233.1 3.1 copy-start.1
  246.1 3.6 copy-start.17
  246.1 3.6 copy-start.25
  253.1 4.3 copy-start.66
  257.4 3.9 copy-start.68
  257.4 3.9 copy-start.8
  257.4 3.9 copy-start.72
  264.1 8.9 %copy-start.79 = (f32[768]{0:T(1024)S(1)}, f32[768]{0:T(1024)}, u32[]{:S(2)}) copy-start(f32[768]{0:T(1024)} %param.35) | copy-start | bytes 9220
  319.8 9.1 %copy-start.76 = (f32[768]{0:T(1024)S(1)}, f32[768]{0:T(1024)}, u32[]{:S(2)}) copy-start(f32[768]{0:T(1024)} %param.37) | copy-start | bytes 9220
  328.9 4.6 copy-start.16
  328.9 4.6 copy-start.23
  339.8 4.7 copy-start.9
  362.1 4.5 copy-start.15
  362.1 11.5 %slice-start.4 = ((s8[6291456]{0:T(1024)(128)(4,1)}), s8[4194304]{0:T(1024)(128)(4,1)S(1)}, s32[]{:S(2)}) async-start(s8[6291456]{0:T(1024)(128)(4,1)} %bitcast.325), calls=%async_computation.4 | async-start | bytes 8388608
  366.6 7.0 %copy-start.44 = (bf16[8,64,768]{2,1,0:T(8,128)(2,1)S(1)}, bf16[8,64,768]{2,1,0:T(8,128)(2,1)}, u32[]{:S(2)}) copy-start(bf16[8,64,768]{2,1,0:T(8,128)(2,1)} %param.23) | copy-start | bytes 2359300
  366.6 7.0 %slice-start.5 = ((s8[6291456]{0:T(1024)(128)(4,1)}), s8[2097152]{0:T(1024)(128)(4,1)S(1)}, s32[]{:S(2)}) async-start(s8[6291456]{0:T(1024)(128)(4,1)} %bitcast.325), calls=%async_computation.5 | async-start | bytes 4194304
  373.6 4.9 copy-start.20
  373.6 4.9 copy-start.32
  510.6 47.9 %copy-start.63 = (f32[192,96]{1,0:T(8,128)S(1)}, f32[192,96]{1,0:T(8,128)}, u32[]{:S(2)}) copy-start(f32[192,96]{1,0:T(8,128)} %get-tuple-element.153) | copy-start | bytes 221188
  510.6 48.5 %copy-start.62 = (f32[192,96]{1,0:T(8,128)S(1)}, f32[192,96]{1,0:T(8,128)}, u32[]{:S(2)}) copy-start(f32[192,96]{1,0:T(8,128)} %get-tuple-element.154) | copy-start | bytes 221188
  510.6 49.2 %copy-start.61 = (f32[192,96]{1,0:T(8,128)S(1)}, f32[192,96]{1,0:T(8,128)}, u32[]{:S(2)}) copy-start(f32[192,96]{1,0:T(8,128)} %get-tuple-element.155) | copy-start | bytes 221188
  510.6 49.8 %copy-start.60 = (f32[192,96]{1,0:T(8,128)S(1)}, f32[192,96]{1,0:T(8,128)}, u32[]{:S(2)}) copy-start(f32[192,96]{1,0:T(8,128)} %get-tuple-element.156) | copy-start | bytes 221188
  510.6 50.4 %copy-start.59 = (f32[192,96]{1,0:T(8,128)S(1)}, f32[192,96]{1,0:T(8,128)}, u32[]{:S(2)}) copy-start(f32[192,96]{1,0:T(8,128)} %get-tuple-element.157) | copy-start | bytes 221188
  510.6 51.1 %copy-start.58 = (f32[192,96]{1,0:T(8,128)S(1)}, f32[192,96]{1,0:T(8,128)}, u32[]{:S(2)}) copy-start(f32[192,96]{1,0:T(8,128)} %get-tuple-element.158) | copy-start | bytes 221188
  512.0 50.3 %copy-start.57 = (f32[192,96]{1,0:T(8,128)S(1)}, f32[192,96]{1,0:T(8,128)}, u32[]{:S(2)}) copy-start(f32[192,96]{1,0:T(8,128)} %get-tuple-element.159) | copy-start | bytes 221188
  512.0 51.0 %copy-start.56 = (f32[192,96]{1,0:T(8,128)S(1)}, f32[192,96]{1,0:T(8,128)}, u32[]{:S(2)}) copy-start(f32[192,96]{1,0:T(8,128)} %get-tuple-element.160) | copy-start | bytes 221188
  512.0 51.6 %copy-start.53 = (f32[192,384]{1,0:T(8,128)S(1)}, f32[192,384]{1,0:T(8,128)}, u32[]{:S(2)}) copy-start(f32[192,384]{1,0:T(8,128)} %get-tuple-element.161) | copy-start | bytes 884740
  (42 other events, 72.9 us)

commit v2 on v0

--- a/solution.py
+++ b/solution.py
@@ -1,12 +1,17 @@
+import functools
+
 import jax
 import jax.numpy as jnp
 from jax import lax
+from jax.experimental import pallas as pl
+from jax.experimental.pallas import tpu as pltpu
 from jax.sharding import PartitionSpec as P
 
 HEADS = 12
 HEAD = 64
-
-
+MESH = pl.DeviceIdType.MESH
+BF = jnp.bfloat16
+F32 = jnp.float32
 EPS = 1e-06
 NEG = -1e30
 
@@ -347,9 +352,1043 @@
     )
 
 
+class Place:
+    def __init__(self):
+        self.d = lax.axis_index("dp")
+        self.m = lax.axis_index("mem")
+        self.c = lax.rem(self.d, 2)
+        self.x = lax.div(self.d, 2)
+        self.y = lax.rem(self.m, 2)
+        self.z = lax.div(self.m, 2)
+        self.oc, self.ox, self.oy = 1 - self.c, 1 - self.x, 1 - self.y
+        self.sib = (self.x * 2 + self.oc, self.m)
+        self.xn = (self.ox * 2 + self.c, self.m)
+        self.yn = (self.d, self.z * 2 + self.oy)
+
+    def zup(self, k):
+        return lax.rem(self.z + k, 4)
+
+    def zpeer(self, k):
+        return (self.d, self.zup(k) * 2 + self.y)
+
+    def mpeer(self, k):
+        return (self.d, lax.rem(self.m + k, 8))
+
+
+def greet(at):
+    barrier = pltpu.get_barrier_semaphore()
+    for peer in [at.sib, at.xn] + [at.mpeer(k) for k in range(1, 8)]:
+        pl.semaphore_signal(barrier, inc=1, device_id=peer, device_id_type=MESH)
+    pl.semaphore_wait(barrier, 9)
+
+
+def remote(src, dst, sends, recvs, idx, peer):
+    return pltpu.make_async_remote_copy(
+        src_ref=src,
+        dst_ref=dst,
+        send_sem=sends.at[idx],
+        recv_sem=recvs.at[idx],
+        device_id=peer,
+        device_id_type=MESH,
+    )
+
+
+class Gather:
+    def __init__(self, at, full, span, sends, recvs, base):
+        self.at, self.full, self.span = at, full, span
+        self.sends, self.recvs, self.base = sends, recvs, base
+        self.lanes = full.shape[-1] // 2
+        self.out = []
+
+    def piece(self, z, y, h, x):
+        lo = pl.multiple_of(x * self.lanes, 128)
+        return self.full.at[self.span, z, y, h, :, pl.ds(lo, self.lanes)]
+
+    def copy(self, slot, src, dst, peer):
+        return remote(src, dst, self.sends, self.recvs, self.base + slot, peer)
+
+    def send(self, slot, src, dst, peer):
+        copy = self.copy(slot, src, dst, peer)
+        copy.start()
+        self.out.append(copy)
+
+    def got(self, slot, ref):
+        self.copy(slot, ref, ref, self.at.sib).wait_recv()
+
+    def begin(self):
+        at = self.at
+        own = self.piece(at.z, at.y, at.c, at.x)
+        for k in (1, 2, 3):
+            self.send(k - 1, own, own, at.zpeer(k))
+        self.send(3, own, own, at.xn)
+        self.send(7, own, own, at.yn)
+        self.send(13, own, own, at.sib)
+
+    def second(self):
+        at = self.at
+        for k in (1, 2, 3):
+            ref = self.piece(at.zup(4 - k), at.y, at.c, at.x)
+            self.got(k - 1, ref)
+            self.send(3 + k, ref, ref, at.xn)
+            self.send(7 + k, ref, ref, at.yn)
+            self.send(13 + k, ref, ref, at.sib)
+
+    def third(self):
+        at = self.at
+        for k in range(4):
+            self.got(3 + k, self.piece(at.zup(4 - k), at.y, at.c, at.ox))
+        ref = self.piece(pl.ds(0, 2), at.y, at.c, at.ox)
+        self.send(11, ref, ref, at.yn)
+        ref = self.piece(slice(None), at.y, at.c, at.ox)
+        self.send(17, ref, ref, at.sib)
+        for k in range(4):
+            self.got(7 + k, self.piece(at.zup(4 - k), at.oy, at.c, at.x))
+        ref = self.piece(pl.ds(2, 2), at.oy, at.c, at.x)
+        self.send(12, ref, ref, at.xn)
+        ref = self.piece(slice(None), at.oy, at.c, at.x)
+        self.send(18, ref, ref, at.sib)
+
+    def fourth(self):
+        at = self.at
+        for half in range(2):
+            ref = self.piece(pl.ds(2 * half, 2), at.oy, at.c, at.ox)
+            self.got(11 + half, ref)
+            self.send(19 + half, ref, ref, at.sib)
+
+    def last(self):
+        at = self.at
+        for k in range(4):
+            self.got(13 + k, self.piece(at.zup(4 - k), at.y, at.oc, at.x))
+        self.got(17, self.piece(slice(None), at.y, at.oc, at.ox))
+        self.got(18, self.piece(slice(None), at.oy, at.oc, at.x))
+        for half in range(2):
+            self.got(19 + half, self.piece(pl.ds(2 * half, 2), at.oy, at.oc, at.ox))
+
+    def drain(self):
+        for copy in self.out:
+            copy.wait_send()
+        self.out = []
+
+
+GATHER_SLOTS = 21
+
+
+class Reduce:
+    def __init__(self, at, sources, parts, mine, bufs, sends, recvs, base):
+        self.at, self.sources, self.parts, self.mine = at, sources, parts, mine
+        self.chip, self.rdiag, self.rx, self.ry, self.rz, self.fin = bufs
+        self.sends, self.recvs, self.base = sends, recvs, base
+        self.count = self.chip.shape[0]
+        self.out = []
+
+    send, got, copy, drain = Gather.send, Gather.got, Gather.copy, Gather.drain
+
+    def begin(self, part):
+        for src, dst in self.sources(part):
+            self.copy(part, src, dst, self.at.sib).start()
+        whole = self.parts(part)
+        self.out.append(self.copy(part, whole, whole, self.at.sib))
+
+    def second(self):
+        at, chip = self.at, self.chip
+        for part in range(2):
+            self.got(part, self.parts(part))
+
+        def add(i, carry):
+            w, r = lax.div(i, 8), lax.rem(i, 8)
+            z, y = lax.div(r, 2), lax.rem(r, 2)
+            for x in range(2):
+                chip[w, x, z, y] = (
+                    chip[w, x, z, y].astype(F32) + self.mine(w, x, z, y).astype(F32)
+                ).astype(BF)
+            return carry
+
+        lax.fori_loop(0, 8 * self.count, add, 0)
+        self.send(2, chip.at[:, at.ox, pl.ds(0, 2), at.oy], self.rdiag.at[0], at.yn)
+        self.send(3, chip.at[:, at.ox, pl.ds(2, 2), at.oy], self.rdiag.at[1], at.xn)
+
+    def third(self):
+        at, chip = self.at, self.chip
+        for half in range(2):
+            self.got(2 + half, self.rdiag.at[half])
+            x, y = ((at.ox, at.y), (at.x, at.oy))[half]
+
+            def add(i, carry, x=x, y=y, half=half):
+                w, z = lax.div(i, 2), lax.rem(i, 2)
+                chip[w, x, 2 * half + z, y] = (
+                    chip[w, x, 2 * half + z, y].astype(F32)
+                    + self.rdiag[half, w, z].astype(F32)
+                ).astype(BF)
+                return carry
+
+            lax.fori_loop(0, 2 * self.count, add, 0)
+        self.send(4, chip.at[:, at.ox, :, at.y], self.rx, at.xn)
+        self.send(5, chip.at[:, at.x, :, at.oy], self.ry, at.yn)
+
+    def fourth(self):
+        at, chip = self.at, self.chip
+        self.got(4, self.rx)
+        self.got(5, self.ry)
+
+        def add(i, carry):
+            w, z = lax.div(i, 4), lax.rem(i, 4)
+            chip[w, at.x, z, at.y] = (
+                chip[w, at.x, z, at.y].astype(F32)
+                + self.rx[w, z].astype(F32)
+                + self.ry[w, z].astype(F32)
+            ).astype(BF)
+            return carry
+
+        lax.fori_loop(0, 4 * self.count, add, 0)
+        for k in (1, 2, 3):
+            self.send(
+                5 + k, chip.at[:, at.x, at.zup(k), at.y], self.rz.at[k - 1], at.zpeer(k)
+            )
+
+    def fifth(self):
+        at = self.at
+        for k in (1, 2, 3):
+            self.got(5 + k, self.rz.at[k - 1])
+
+        def add(w, carry):
+            total = self.chip[w, at.x, at.z, at.y].astype(F32)
+            for k in range(3):
+                total = total + self.rz[k, w].astype(F32)
+            self.fin[at.c, w] = total.astype(BF)
+            return carry
+
+        lax.fori_loop(0, self.count, add, 0)
+        self.send(9, self.fin.at[at.c], self.fin.at[at.c], at.sib)
+
+    def last(self):
+        self.got(9, self.fin.at[self.at.oc])
+
+
+REDUCE_SLOTS = 10
+
+
+def reduce_bufs(count, rows, lanes):
+    return [
+        pltpu.VMEM((count, 2, 4, 2, rows, lanes), BF),
+        pltpu.VMEM((2, count, 2, rows, lanes), BF),
+        pltpu.VMEM((count, 4, rows, lanes), BF),
+        pltpu.VMEM((count, 4, rows, lanes), BF),
+        pltpu.VMEM((3, count, rows, lanes), BF),
+        pltpu.VMEM((2, count, rows, lanes), BF),
+    ]
+
+
+def pick(rows, cols, start):
+    col = lax.broadcasted_iota(jnp.int32, (rows, cols), 1)
+    row = lax.broadcasted_iota(jnp.int32, (rows, cols), 0)
+    return jnp.where(col == row + start, 1.0, 0.0).astype(BF)
+
+
+def dot_nt(a, b):
+    return lax.dot_general(a, b, (((1,), (1,)), ((), ())), preferred_element_type=F32)
+
+
+def dot_nn(a, b):
+    return lax.dot_general(a, b, (((1,), (0,)), ((), ())), preferred_element_type=F32)
+
+
+def dot_tn(a, b):
+    return lax.dot_general(a, b, (((0,), (0,)), ((), ())), preferred_element_type=F32)
+
+
+def norm_stats(values):
+    center = values - jnp.mean(values, axis=-1, keepdims=True)
+    scale = lax.rsqrt(jnp.mean(center * center, axis=-1, keepdims=True) + EPS)
+    return center * scale, scale
+
+
+def gelu_both(value):
+    c0, c1 = 0.7978845608028654, 0.044715
+    square = value * value
+    tanh = jnp.tanh(c0 * value * (1.0 + c1 * square))
+    half = 0.5 + 0.5 * tanh
+    slope = half + 0.5 * value * (1.0 - tanh * tanh) * (c0 + 3.0 * c0 * c1 * square)
+    return value * half, slope
+
+
+def softmax(scores):
+    powered = jnp.exp(scores - jnp.max(scores, axis=-1, keepdims=True))
+    return powered / jnp.sum(powered, axis=-1, keepdims=True)
+
+
+class Layer:
+    def __init__(self, **refs):
+        self.__dict__.update(refs)
+        self.tokens, self.dmodel = self.nrm.shape
+        self.images = self.own_images
+        self.txt = self.tokens // self.images
+        self.mem_len = self.mk.shape[0] // self.images
+        lane = lax.broadcasted_iota(jnp.int32, (1, 4 * HEAD), 1)
+        self.head_lanes = [
+            jnp.where((lane >= HEAD * h) & (lane < HEAD * (h + 1)), 1.0, 0.0)
+            for h in range(4)
+        ]
+
+    def weight(self, i):
+        return self.full_s[i].reshape(self.dmodel, self.dmodel)
+
+    def put_weight(self, i, value):
+        self.full_s[i] = value.astype(BF).reshape(self.full_s.shape[1:])
+
+    def blocks(self, size, fn, total=None):
+        def step(i, carry):
+            fn(pl.ds(pl.multiple_of(i * size, size), size))
+            return carry
+
+        lax.fori_loop(0, (total or self.tokens) // size, step, 0)
+
+    def spread(self, value):
+        return jnp.concatenate(
+            [value * mask.astype(BF) for mask in self.head_lanes], axis=0
+        )
+
+    def gather_heads(self, value):
+        n = value.shape[0] // 4
+        out = value[:n] * self.head_lanes[0]
+        for h in range(1, 4):
+            out = out + value[h * n : (h + 1) * n] * self.head_lanes[h]
+        return out
+
+    def norm_into(self, source, index):
+        gain, shift = self.norms[2 * index : 2 * index + 1], self.norms[2 * index + 1 : 2 * index + 2]
+
+        def block(rows):
+            hat, _ = norm_stats(source[rows, :].astype(F32))
+            self.nrm[rows, :] = (hat * gain + shift).astype(BF)
+
+        self.blocks(128, block)
+
+    def norm_back(self, source, upstream, index, finish):
+        gain = self.norms[2 * index : 2 * index + 1]
+
+        def step(i, carry):
+            rows = pl.ds(pl.multiple_of(i * 64, 64), 64)
+            hat, scale = norm_stats(source[rows, :].astype(F32))
+            up = upstream[rows, :]
+            scaled = up * gain
+            first = jnp.mean(scaled, axis=-1, keepdims=True)
+            second = jnp.mean(scaled * hat, axis=-1, keepdims=True)
+            finish(rows, scale * (scaled - first - hat * second))
+            gains, shifts = carry
+            return (
+                gains + jnp.sum(up * hat, axis=0, keepdims=True),
+                shifts + jnp.sum(up, axis=0, keepdims=True),
+            )
+
+        zero = jnp.zeros((1, self.dmodel), F32)
+        gains, shifts = lax.fori_loop(0, self.tokens // 64, step, (zero, zero))
+        self.norm_grads[2 * index : 2 * index + 1, :] = gains
+        self.norm_grads[2 * index + 1 : 2 * index + 2, :] = shifts
+
+
+    def project(self, out, source, i):
+        out[...] = dot_nt(source[...], self.weight(i)).astype(BF)
+
+    def self_forward(self):
+        def pair(p, carry):
+            rows = pl.ds(pl.multiple_of(p * 128, 128), 128)
+            allow = self.allow[p].astype(F32)
+            for g in range(self.dmodel // 256):
+                cols = slice(256 * g, 256 * g + 256)
+                scores = dot_nt(self.spread(self.q[rows, cols]), self.k[rows, cols])
+                scores = scores.reshape(4, 128, 128) * HEAD**-0.5
+                scores = jnp.where((allow > 0.5)[None], scores, NEG)
+                probs = softmax(scores).reshape(512, 128).astype(BF)
+                self.ps[p, g] = probs
+                mixed = dot_nn(probs, self.v[rows, cols])
+                self.sm[rows, cols] = self.gather_heads(mixed).astype(BF)
+            return carry
+
+        lax.fori_loop(0, self.images // 2, pair, 0)
+
+    def add_after_self(self):
+        def block(rows):
+            self.after_self[rows, :] = self.io[rows, :].astype(F32) + dot_nt(
+                self.sm[rows, :], self.weight(3)
+            )
+
+        self.blocks(256, block)
+
+    def swap_rows(self, out, source):
+        n, size = self.images, self.mem_len
+        short = size // n
+        total = n * size
+
+        def block(i, carry):
+            row = lax.broadcasted_iota(jnp.int32, (size, total), 0)
+            col = lax.broadcasted_iota(jnp.int32, (size, total), 1)
+            which = jnp.floor((row.astype(F32) + 0.5) * (1.0 / short)).astype(jnp.int32)
+            hit = col == row + which * (size - short) + i * short
+            rows = pl.ds(pl.multiple_of(i * size, 32), size)
+            out[rows, :] = dot_nn(jnp.where(hit, 1.0, 0.0).astype(BF), source[...]).astype(BF)
+            return carry
+
+        lax.fori_loop(0, n, block, 0)
+
+    def memory_in(self):
+        self.swap_rows(self.mk, self.rows)
+        self.rows[...] = self.mk[...]
+
+    def probs_at(self, i, g):
+        size = 4 * self.txt
+        start = pl.multiple_of(lax.rem(i, 2) * size, size)
+        return lax.div(i, 2), g, pl.ds(start, size), slice(0, self.mem_len)
+
+    def cross_forward(self):
+        def image(i, carry):
+            rows = pl.ds(pl.multiple_of(i * self.txt, 64), self.txt)
+            mems = pl.ds(pl.multiple_of(i * self.mem_len, 32), self.mem_len)
+            for g in range(self.dmodel // 256):
+                cols = slice(256 * g, 256 * g + 256)
+                scores = dot_nt(self.spread(self.cq[rows, cols]), self.mk[mems, cols])
+                probs = softmax(scores * HEAD**-0.5).astype(BF)
+                self.ps[self.probs_at(i, g)] = probs
+                mixed = dot_nn(probs, self.mv[mems, cols])
+                self.cm[rows, cols] = self.gather_heads(mixed).astype(BF)
+            return carry
+
+        lax.fori_loop(0, self.images, image, 0)
+
+    def add_after_cross(self):
+        def block(rows):
+            self.after_cross[rows, :] = self.after_self[rows, :] + dot_nt(
+                self.cm[rows, :], self.weight(7)
+            )
+
+        self.blocks(256, block)
+
+
+    def mask_top(self):
+        def block(rows):
+            self.io[rows, :] = self.io[rows, :] * self.valid[rows, :1]
+
+        self.blocks(128, block)
+
+    def feed_start(self):
+        def block(rows):
+            self.acc_out[rows, :] = self.after_cross[rows, :]
+            self.acc_up[rows, :] = jnp.zeros((128, self.dmodel), F32)
+
+        self.blocks(128, block)
+
+    def feed_chunk(self, z):
+        dmodel = self.dmodel
+        lo = pl.multiple_of(z * dmodel, 128)
+
+        def w_out():
+            return self.full_out[0, :, :, :, :, pl.ds(lo, dmodel)].reshape(dmodel, dmodel)
+
+        def w_in():
+            return self.full_in[0, z].reshape(dmodel, dmodel)
+
+        def block(rows):
+            before = dot_nt(self.nrm[rows, :], w_in())
+            act, slope = gelu_both(before)
+            self.t2[rows, :] = act.astype(BF)
+            up = dot_nn(self.io[rows, :], w_out())
+            self.t3[rows, :] = (slope * up).astype(BF)
+
+        self.blocks(256, block)
+
+        def block(rows):
+            self.acc_out[rows, :] += dot_nt(self.t2[rows, :], w_out())
+            self.acc_up[rows, :] += dot_nn(self.t3[rows, :], w_in())
+
+        self.blocks(256, block)
+        self.full_out[0, :, :, :, :, pl.ds(lo, dmodel)] = (
+            dot_tn(self.io[...], self.t2[...]).astype(BF)
+        ).reshape(self.full_out.shape[1:5] + (dmodel,))
+        self.full_in[0, z] = (
+            dot_tn(self.t3[...], self.nrm[...]).astype(BF).reshape(self.full_in.shape[2:])
+        )
+
+    def layer_out(self, out):
+        def block(rows):
+            out[rows, :] = (self.acc_out[rows, :] * self.valid[rows, :1].astype(F32)).astype(BF)
+
+        self.blocks(128, block)
+
+
+    def third_back(self):
+        def finish(rows, grad):
+            total = self.io[rows, :].astype(F32) + grad
+            self.acc_up[rows, :] = total
+            self.io[rows, :] = total.astype(BF)
+
+        self.norm_back(self.after_cross, self.acc_up, 2, finish)
+
+    def output_back(self, i, mixed, out):
+        out[...] = dot_nn(self.io[...], self.weight(i)).astype(BF)
+        self.put_weight(i, dot_tn(self.io[...], mixed[...]))
+
+    def attend_back(self, probs, up, q, k, v, rows, mems, cols):
+        low_q = self.spread(q[rows, cols])
+        low_up = self.spread(up[rows, cols])
+        keys, values = k[mems, cols], v[mems, cols]
+        full = probs.astype(F32)
+        prob_grad = dot_nt(low_up, values)
+        score = full * (prob_grad - jnp.sum(prob_grad * full, axis=-1, keepdims=True))
+        score = (score * HEAD**-0.5).astype(BF)
+        v[mems, cols] = dot_tn(probs, low_up).astype(BF)
+        k[mems, cols] = dot_tn(score, low_q).astype(BF)
+        q[rows, cols] = self.gather_heads(dot_nn(score, keys)).astype(BF)
+
+    def cross_back(self, start, stop):
+        def image(i, carry):
+            rows = pl.ds(pl.multiple_of(i * self.txt, 64), self.txt)
+            mems = pl.ds(pl.multiple_of(i * self.mem_len, 32), self.mem_len)
+            for g in range(self.dmodel // 256):
+                cols = slice(256 * g, 256 * g + 256)
+                probs = self.ps[self.probs_at(i, g)]
+                self.attend_back(
+                    probs, self.t2, self.cq, self.mk, self.mv, rows, mems, cols
+                )
+            return carry
+
+        lax.fori_loop(start, stop, image, 0)
+
+    def self_back(self):
+        def pair(p, carry):
+            rows = pl.ds(pl.multiple_of(p * 128, 128), 128)
+            for g in range(self.dmodel // 256):
+                cols = slice(256 * g, 256 * g + 256)
+                self.attend_back(
+                    self.ps[p, g], self.t2, self.q, self.k, self.v, rows, rows, cols
+                )
+            return carry
+
+        lax.fori_loop(0, self.images // 2, pair, 0)
+
+    def memory_back(self):
+        key_grad = dot_tn(self.mk[...], self.rows[...])
+
+        def block(rows):
+            total = dot_nn(self.mk[rows, :], self.weight(5)) + dot_nn(
+                self.mv[rows, :], self.weight(6)
+            )
+            self.back[rows, :] = total.astype(BF)
+
+        self.blocks(256, block, self.mk.shape[0])
+        self.put_weight(5, key_grad)
+        self.put_weight(6, dot_tn(self.mv[...], self.rows[...]))
+        self.swap_rows(self.rows, self.back)
+
+    def second_up(self):
+        def block(rows):
+            self.acc_out[rows, :] = dot_nn(self.cq[rows, :], self.weight(4))
+
+        self.blocks(256, block)
+
+    def query_grad(self):
+        self.put_weight(4, dot_tn(self.cq[...], self.nrm[...]))
+
+    def second_back(self):
+        def finish(rows, grad):
+            total = self.acc_up[rows, :] + grad
+            self.acc_up[rows, :] = total
+            self.io[rows, :] = total.astype(BF)
+
+        self.norm_back(self.after_self, self.acc_out, 1, finish)
+
+    def first_up(self):
+        def block(rows):
+            self.acc_out[rows, :] = (
+                dot_nn(self.q[rows, :], self.weight(0))
+                + dot_nn(self.k[rows, :], self.weight(1))
+                + dot_nn(self.v[rows, :], self.weight(2))
+            )
+
+        self.blocks(256, block)
+
+    def first_grads(self):
+        for i, low in enumerate((self.q, self.k, self.v)):
+            self.put_weight(i, dot_tn(low[...], self.nrm[...]))
+
+    def first_back(self, text, out):
+        def finish(rows, grad):
+            out[rows, :] = (self.acc_up[rows, :] + grad).astype(BF)
+
+        self.norm_back(text, self.acc_out, 0, finish)
+
+
+class NormSum:
+    def __init__(self, at, sums, recv, sends, recvs):
+        self.at, self.sums, self.recv, self.sends, self.recvs = at, sums, recv, sends, recvs
+        flip = (at.d, (at.z + 1 - 2 * lax.rem(at.z, 2)) * 2 + at.y)
+        self.peers = [at.sib, at.xn, at.yn, flip, at.zpeer(2)]
+        self.out = []
+
+    def start(self, i):
+        copy = remote(
+            self.sums.at[i], self.recv.at[i], self.sends, self.recvs, i, self.peers[i]
+        )
+        copy.start()
+        self.out.append(copy)
+
+    def finish(self, i):
+        self.out[i].wait_recv()
+        self.sums[i + 1] = self.sums[i] + self.recv[i]
+
+
+REDUCE_COUNTS = (4, 4, 1, 3, 1, 3)
+NAMES = ("nrm", "io", "q", "k", "v", "sm", "cq", "cm", "t2", "t3")
+WIDE = ("after_self", "after_cross", "acc_out", "acc_up")
+
+
+def whole_kernel(own_images, *refs):
+    refs = list(refs)
+
+    def take(n):
+        out = refs[:n]
+        del refs[:n]
+        return out
+
+    shards, (rows_in, text_in, top_in) = take(10), take(3)
+    valid, allow, norms = take(3)
+    outs, (layer_out, text_out, rows_out, norm_out, spill) = take(10), take(5)
+    full_s, full_in, full_out, pair_s, pair_in, pair_out = take(6)
+    bufs = [take(6) for _ in REDUCE_COUNTS]
+    narrow, wide = take(len(NAMES)), take(len(WIDE))
+    rows, mk, mv, ps, norm_sums, norm_recv = take(6)
+    (psend, precv, gsend, grecv, hsend, hrecv, rsend, rrecv, bsend, brecv, nsend, nrecv, local) = refs
+    at = Place()
+    greet(at)
+    layer = Layer(
+        own_images=own_images,
+        full_s=full_s,
+        full_in=full_in,
+        full_out=full_out,
+        rows=rows,
+        mk=mk,
+        mv=mv,
+        ps=ps,
+        back=mk,
+        valid=valid,
+        allow=allow,
+        norms=norms,
+        norm_grads=norm_sums.at[0],
+        **dict(zip(NAMES, narrow)),
+        **dict(zip(WIDE, wide)),
+    )
+
+    pairs = [pair_s.at[i] for i in range(8)] + [pair_in, pair_out]
+    own, other = [], []
+    for i in range(10):
+        depth = shards[i].shape[0]
+        mine = pairs[i].at[pl.ds(pl.multiple_of(at.c * depth, 8), depth), :]
+        copy = remote(shards[i], mine, psend, precv, i, at.sib)
+        copy.start()
+        other.append(copy)
+        copy = pltpu.make_async_copy(shards[i], mine, local.at[i])
+        copy.start()
+        own.append(copy)
+    load = pltpu.make_async_copy(text_in, layer.io, local.at[10])
+    load.start()
+
+    def ready(i):
+        own[i].wait()
+        depth = shards[i].shape[0]
+        theirs = pairs[i].at[pl.ds(pl.multiple_of(at.oc * depth, 8), depth), :]
+        remote(theirs, theirs, psend, precv, i, at.sib).wait_recv()
+
+    def lay_in(full, w, i, half, lanes):
+        ready(i)
+        lo = pl.multiple_of(at.x * lanes, 128)
+        block = dot_nt(pick(half, 2 * half, at.c * half), pairs[i][...])
+        full[w, at.z, at.y, at.c, :, pl.ds(lo, lanes)] = block.astype(BF)
+
+    fulls = (full_s, full_s, full_in, full_out)
+    spans = (slice(0, 3), slice(3, 8), slice(0, 1), slice(0, 1))
+    groups = [
+        Gather(at, full, span, gsend, grecv, GATHER_SLOTS * g)
+        for g, (full, span) in enumerate(zip(fulls, spans))
+    ]
+    for g, group in enumerate(groups):
+        half, lanes = group.full.shape[4], group.full.shape[5] // 2
+        for w in range(group.span.start, group.span.stop):
+            lay_in(group.full, w, w if g < 2 else 6 + g, half, lanes)
+        group.begin()
+    size = rows.shape[0] // 8
+
+    def block_of(m):
+        return rows.at[pl.ds(pl.multiple_of(m * size, 32), size), :]
+
+    mems = []
+    for k in range(1, 8):
+        to = lax.rem(at.m + k, 8)
+        copy = remote(rows_in.at[to], block_of(at.m), rsend, rrecv, k - 1, at.mpeer(k))
+        copy.start()
+        mems.append(copy)
+    keep = pltpu.make_async_copy(rows_in.at[at.m], block_of(at.m), local.at[11])
+    keep.start()
+
+    first, rest, feed_in, feed_out = groups
+    load.wait()
+    layer.norm_into(layer.io, 0)
+    first.second()
+    rest.second()
+    first.third()
+    feed_in.second()
+    first.fourth()
+    feed_out.second()
+    first.last()
+    layer.project(layer.q, layer.nrm, 0)
+    rest.third()
+    layer.project(layer.k, layer.nrm, 1)
+    layer.project(layer.v, layer.nrm, 2)
+    feed_in.third()
+    rest.fourth()
+    layer.self_forward()
+    away = pltpu.make_async_copy(ps, spill, local.at[13])
+    away.start()
+    rest.last()
+    layer.add_after_self()
+    feed_out.third()
+    feed_in.fourth()
+    top = pltpu.make_async_copy(top_in, layer.io, local.at[10])
+    top.start()
+    layer.norm_into(layer.after_self, 1)
+    layer.project(layer.cq, layer.nrm, 4)
+    keep.wait()
+    for k in range(1, 8):
+        ref = block_of(lax.rem(at.m + 8 - k, 8))
+        remote(ref, ref, rsend, rrecv, k - 1, at.sib).wait_recv()
+    layer.memory_in()
+    layer.project(layer.mk, layer.rows, 5)
+    layer.project(layer.mv, layer.rows, 6)
+    feed_out.fourth()
+    away.wait()
+    layer.cross_forward()
+    layer.add_after_cross()
+    layer.norm_into(layer.after_cross, 2)
+    top.wait()
+    layer.mask_top()
+    layer.feed_start()
+    feed_in.last()
+    feed_out.last()
+    for copy in other + mems:
+        copy.wait_send()
+    for group in groups:
+        group.drain()
+
+    half, dmodel = full_s.shape[4:]
+    lanes = dmodel // 2
+
+    def small(g, span):
+        chip, w0 = bufs[g][0], span.start
+
+        def sources(part):
+            cut = slice(part * lanes, (part + 1) * lanes)
+            return [(full_s.at[span, :, :, at.oc, :, cut], chip.at[:, part])]
+
+        def mine(w, x, z, y):
+            return full_s[w0 + w, z, y, at.c, :, x * lanes : (x + 1) * lanes]
+
+        return Reduce(
+            at, sources, lambda x: chip.at[:, x], mine, bufs[g], hsend, hrecv, REDUCE_SLOTS * g
+        )
+
+    def out_group(g):
+        chip = bufs[g][0]
+        count = chip.shape[0]
+
+        def cut(j, x):
+            lo = (x * count + j) * lanes
+            return slice(lo, lo + lanes)
+
+        def sources(x):
+            return [
+                (full_out.at[0, :, :, at.oc, :, cut(j, x)], chip.at[j, x])
+                for j in range(count)
+            ]
+
+        def mine(j, x, z, y):
+            lo = pl.multiple_of((x * count + j) * lanes, 128)
+            return full_out[0, z, y, at.c, :, pl.ds(lo, lanes)]
+
+        return Reduce(
+            at, sources, lambda x: chip.at[:, x], mine, bufs[g], hsend, hrecv, REDUCE_SLOTS * g
+        )
+
+    def in_group(g):
+        chip = bufs[g][0]
+        count = chip.shape[0]
+
+        def sources(part):
+            zs = pl.ds(2 * part, 2)
+            return [
+                (
+                    full_in.at[
+                        0, zs, :, at.oc, s * half : (s + 1) * half, x * lanes : (x + 1) * lanes
+                    ],
+                    chip.at[s, x, zs],
+                )
+                for s in range(count)
+                for x in range(2)
+            ]
+
+        def mine(s, x, z, y):
+            lo = pl.multiple_of(s * half, 16)
+            return full_in[0, z, y, at.c, pl.ds(lo, half), x * lanes : (x + 1) * lanes]
+
+        def parts(part):
+            return chip.at[:, :, pl.ds(2 * part, 2)]
+
+        return Reduce(at, sources, parts, mine, bufs[g], hsend, hrecv, REDUCE_SLOTS * g)
+
+    g_out, g_in = out_group(0), in_group(1)
+    g_co, g_cross = small(2, slice(7, 8)), small(3, slice(4, 7))
+    g_so, g_self = small(4, slice(3, 4)), small(5, slice(0, 3))
+
+    def chunks(a, b):
+        def step(z, carry):
+            layer.feed_chunk(z)
+            return carry
+
+        lax.fori_loop(a, b, step, 0)
+
+    chunks(0, 2)
+    g_out.begin(0)
+    g_in.begin(0)
+    chunks(2, 4)
+    g_out.begin(1)
+    g_in.begin(1)
+    layer.layer_out(layer.t3)
+    save = pltpu.make_async_copy(layer.t3, layer_out, local.at[12])
+    save.start()
+    g_out.second()
+    layer.third_back()
+    g_in.second()
+    layer.output_back(7, layer.cm, layer.t2)
+    g_co.begin(0)
+    g_co.begin(1)
+    g_out.third()
+    layer.cross_back(0, own_images // 2)
+    g_in.third()
+    g_co.second()
+    layer.cross_back(own_images // 2, own_images)
+    again = pltpu.make_async_copy(spill, ps, local.at[13])
+    again.start()
+    g_out.fourth()
+    g_co.third()
+    layer.second_up()
+    layer.norm_into(layer.after_self, 1)
+    layer.query_grad()
+    layer.memory_back()
+    g_cross.begin(0)
+    g_cross.begin(1)
+    backs = []
+    for k in range(1, 8):
+        to = lax.rem(at.m + k, 8)
+        copy = remote(block_of(to), rows_out.at[at.m], bsend, brecv, k - 1, at.mpeer(k))
+        copy.start()
+        backs.append(copy)
+    keep = pltpu.make_async_copy(block_of(at.m), rows_out.at[at.m], local.at[11])
+    keep.start()
+    layer.second_back()
+    g_in.fourth()
+    layer.output_back(3, layer.sm, layer.t2)
+    g_so.begin(0)
+    g_so.begin(1)
+    g_cross.second()
+    text = pltpu.make_async_copy(text_in, layer.sm, local.at[10])
+    text.start()
+    again.wait()
+    layer.self_back()
+    g_so.second()
+    g_co.fourth()
+    g_cross.third()
+    text.wait()
+    layer.norm_into(layer.sm, 0)
+    layer.first_up()
+    layer.first_grads()
+    g_self.begin(0)
+    g_self.begin(1)
+    g_so.third()
+    save.wait()
+    layer.first_back(layer.sm, layer.t3)
+    save = pltpu.make_async_copy(layer.t3, text_out, local.at[12])
+    save.start()
+    norm = NormSum(at, norm_sums, norm_recv, nsend, nrecv)
+    norm.start(0)
+    g_self.second()
+    norm.finish(0)
+    norm.start(1)
+    g_out.fifth()
+    g_in.fifth()
+    g_cross.fourth()
+    norm.finish(1)
+    norm.start(2)
+    g_self.third()
+    g_co.fifth()
+    g_so.fourth()
+    norm.finish(2)
+    norm.start(3)
+    depth = shards[0].shape[0]
+
+    def lay(out, blocks):
+        both = jnp.concatenate(blocks, axis=0)
+        rows_ = out.shape[0]
+        out[...] = dot_nt(pick(rows_, both.shape[1], at.c * rows_), both).astype(BF)
+
+    def lay_small(group, start):
+        group.last()
+        for w in range(group.count):
+            lay(outs[start + w], [group.fin[0, w], group.fin[1, w]])
+
+    g_out.last()
+    count = g_out.count
+    lay(
+        outs[9],
+        [
+            jnp.concatenate([g_out.fin[h, j] for j in range(count)], axis=1)
+            for h in range(2)
+        ],
+    )
+    g_in.last()
+    lay(outs[8], [g_in.fin[h, s] for h in range(2) for s in range(count)])
+    norm.finish(3)
+    norm.start(4)
+    g_cross.fifth()
+    g_so.fifth()
+    lay_small(g_co, 7)
+    g_self.fourth()
+    norm.finish(4)
+    norm_out[...] = norm_sums[5]
+    lay_small(g_cross, 4)
+    lay_small(g_so, 3)
+    g_self.fifth()
+    lay_small(g_self, 0)
+    save.wait()
+    keep.wait()
+    for k in range(1, 8):
+        ref = rows_out.at[lax.rem(at.m + 8 - k, 8)]
+        remote(ref, ref, bsend, brecv, k - 1, at.sib).wait_recv()
+    for copy in backs + norm.out:
+        copy.wait_send()
+    for group in (g_out, g_in, g_co, g_cross, g_so, g_self):
+        group.drain()
+
+
+def whole(shards, rows, text, top, valid, allow, norms, own_images):
+    depth, width = shards[0].shape
+    dmodel = depth * 4
+    half = width // 2
+    half_in = shards[8].shape[1] // 2
+    ff = half_in * 16
+    shapes = [
+        (8, 4, 2, 2, half, dmodel),
+        (1, 4, 2, 2, half_in, dmodel),
+        (1, 4, 2, 2, half, ff),
+    ]
+    tokens = text.shape[0]
+    mem_rows = rows.shape[0] * rows.shape[1]
+    groups = dmodel // 256
+    any_ = pl.BlockSpec(memory_space=pl.ANY)
+    vmem = pl.BlockSpec(memory_space=pltpu.VMEM)
+    sems = pltpu.SemaphoreType.DMA
+    scratch = [pltpu.VMEM(s, BF) for s in shapes]
+    scratch += [
+        pltpu.VMEM((8, 2 * depth, width), BF),
+        pltpu.VMEM((2 * depth, 2 * half_in), BF),
+        pltpu.VMEM((ff // 2, width), BF),
+    ]
+    for count in REDUCE_COUNTS:
+        scratch += reduce_bufs(count, half, dmodel // 2)
+    scratch += [pltpu.VMEM((tokens, dmodel), BF) for _ in NAMES]
+    scratch += [pltpu.VMEM((tokens, dmodel), F32) for _ in WIDE]
+    scratch += [
+        pltpu.VMEM((mem_rows, dmodel), BF),
+        pltpu.VMEM((mem_rows, dmodel), BF),
+        pltpu.VMEM((mem_rows, dmodel), BF),
+        pltpu.VMEM((own_images // 2, groups, 512, 128), BF),
+        pltpu.VMEM((6, 8, dmodel), F32),
+        pltpu.VMEM((5, 8, dmodel), F32),
+    ]
+    for n in (10, 4 * GATHER_SLOTS, len(REDUCE_COUNTS) * REDUCE_SLOTS, 7, 7, 5):
+        scratch += [sems((n,)), sems((n,))]
+    scratch += [sems((14,))]
+    return pl.pallas_call(
+        functools.partial(whole_kernel, own_images),
+        out_shape=[jax.ShapeDtypeStruct(s.shape, BF) for s in shards]
+        + [
+            jax.ShapeDtypeStruct(text.shape, BF),
+            jax.ShapeDtypeStruct(text.shape, BF),
+            jax.ShapeDtypeStruct(rows.shape, BF),
+            jax.ShapeDtypeStruct((8, dmodel), F32),
+            jax.ShapeDtypeStruct((own_images // 2, groups, 512, 128), BF),
+        ],
+        in_specs=[any_] * 13 + [vmem] * 3,
+        out_specs=[vmem] * 10 + [any_] * 3 + [vmem, any_],
+        scratch_shapes=scratch,
+        compiler_params=pltpu.CompilerParams(
+            collective_id=0, has_side_effects=True, vmem_limit_bytes=63 << 20
+        ),
+    )(*shards, rows, text, top, valid, allow, norms)
+
+
+def fits(mesh_shape, text, memory, mats):
+    images, txt, dmodel = text.shape
+    depth, width = mats[0].shape
+    return (
+        mesh_shape["dp"] == 4
+        and mesh_shape["mem"] == 8
+        and images == 8
+        and txt == HEAD == 64
+        and memory.shape[0] == 8 * images
+        and (memory.shape[1] * 8) % 32 == 0
+        and dmodel == HEADS * HEAD == 4 * depth == 8 * width
+        and dmodel % 256 == 0
+        and width % 32 == 0
+        and mats[8].shape == (depth, 4 * width)
+        and mats[9].shape == (4 * depth, width)
+    )
+
+
+def shards_lean(text, lengths, memory, out_grad, *params):
+    mats, norms = params[:10], params[10:]
+    images, txt, dmodel = text.shape
+    tokens = images * txt
+    valid = jnp.arange(txt)[None, :] < lengths[:, None]
+    place = jnp.arange(2 * txt)
+    causal = (place[None, :] // txt == place[:, None] // txt) & (
+        place[None, :] <= place[:, None]
+    )
+    allow = causal[None] & valid.reshape(images // 2, 1, 2 * txt)
+    spread = jnp.broadcast_to(valid.reshape(tokens, 1), (tokens, 128))
+    rows = memory.reshape(8, -1, dmodel)
+    *weight_sums, layer_out, text_grad, back, norm_sums, _ = whole(
+        mats,
+        rows,
+        text.reshape(tokens, dmodel),
+        out_grad.reshape(tokens, dmodel),
+        spread.astype(BF),
+        allow.astype(BF),
+        jnp.stack(norms + norms[:2]),
+        images,
+    )
+    return (
+        layer_out.reshape(text.shape),
+        text_grad.reshape(text.shape),
+        back.reshape(memory.shape),
+        *(total.astype(F32) for total in weight_sums),
+        *(norm_sums[i] for i in range(6)),
+    )
+
+
 def solution(mesh):
+    def pick_form(text, lengths, memory, out_grad, *params):
+        lean = fits(mesh.shape, text, memory, params[:10])
+        form = shards_lean if lean else shards
+        return form(text, lengths, memory, out_grad, *params)
+
     return jax.shard_map(
-        shards,
+        pick_form,
         mesh=mesh,
         in_specs=(
             P(("dp", "mem"), None, None),

time: 1370 us -> 302 us (0.22)
  waiting for transfers between devices: 779 us -> 0 us
  blocking collectives: 295 us -> 0 us
  Pallas kernels: 0 us -> 267 us
  matrix products: 143 us -> 0 us
  local copies, waits for them, and re-layouts: 98.5 us -> 18 us
  between operations: 15.5 us -> 0.74 us
    unnamed x42 -> x0, waiting for transfers between devices: 498 us -> none
    pallas_call x0 -> x1, Pallas kernels: none -> 267 us  [whole(): pl.pallas_call(functools.partial(whole_kernel, own_images), out_shape=[ja...]
    reduce_scatter x10 -> x0, waiting for transfers between devices: 263 us -> none  [the longest x1 62.1 us: reduce_all(): lax.psum_scatter(row_sums[6].astype(jnp.bfloat16), 'mem', scatter_dimensi...]
    all_gather x8 -> x0, blocking collectives: 254 us -> none  [the longest x1 33.3 us: fetch_weights(): lax.all_gather(mats[0], 'mem', axis=1, tiled=True)]
    dot_general x42 -> x0, matrix products: 143 us -> none  [the longest x10 41.2 us: apply_mat(): jnp.einsum('bsd,de->bse', acts, matrix, preferred_element_type=jnp.float32)]
    unnamed x160 -> x14, local copies, waits for them, and re-layouts: 51.9 us -> 8.17 us
    psum x1 -> x0, blocking collectives: 40.6 us -> none  [shards(): lax.psum((first_gain_grad, first_shift_grad, second_gain_grad, second_shi...]
    convert_element_type x9 -> x1, local copies, waits for them, and re-layouts: 19.6 us -> 0.09 us  [shards_lean(): spread.astype(BF)]
  transfers between devices with their start and end apart: 34 -> 0, of which waited for: 18 -> 0; matrix products, arithmetic and copies ran while one was open for 17% -> 0% of each run, Pallas kernels for 0% -> 0%
where the time goes in v2:
time: 302 us; the launch traced here: 300 us
  Pallas kernels  267 us (88%)
  local copies, waits for them, and re-layouts  18 us (6%)
  other arithmetic  14.7 us (5%)
    pallas_call x1, Pallas kernels, whole(): pl.pallas_call(functools.partial(whole_kernel, own_images), out_shape=[ja...  267 us
    convert_element_type x9, other arithmetic, shards_lean(): total.astype(F32)  13.2 us
    unnamed x14, local copies, waits for them, and re-layouts  8.17 us

profile of v2, /device:TPU:0, one launch (start us, length us, event | category | flops | bytes accessed | tf_op | source)
XLA Modules:
  0.0 300.5 jit_solution(11369367694552802610)
XLA Ops:
  0.7 0.1 lt.40
  0.8 0.7 lt.42
  1.5 0.1 lt.43
  1.6 0.1 lt.44
  1.7 0.7 fusion.1
  2.4 0.1 reshape.211
  2.5 0.7 stack.23
  3.2 0.7 stack.24
  3.9 0.7 stack.25
  4.5 0.7 stack.26
  5.2 0.7 stack.27
  5.9 0.7 stack.28
  6.6 0.6 stack.29.refs_15_
  7.3 0.1 fusion
  7.4 0.7 and_convert_fusion.refs_14_
  8.0 0.8 broadcast_in_dim.2.refs_13_
  8.8 1.7 copy.44.refs_9_
  10.6 1.9 copy.43
  12.5 1.2 reshape.205.refs_10_
  13.6 267.0 %shard_map.339 = (bf16[192,96]{1,0:T(8,128)(2,1)}, bf16[192,96]{1,0:T(8,128)(2,1)}, bf16[192,96]{1,0:T(8,128)(2,1)}, bf16[192,96]{1,0:T(8,128)(2,1)}, bf16[192,9...) custom-call(bf16[192,96]{1,0:T(8,128)(2,1)} %refs_0_.1, ...), custom_call_target="tpu_custom_call" | custom-call | tf_op jit(solution)/shard_map/pallas_call | solution.py:1316
  280.7 0.0 copy-start.3
  280.7 0.0 copy-start
  280.7 1.7 slice_reduce_fusion
  282.4 1.4 convert_element_type.41
  283.9 1.4 convert_element_type.42
  285.3 1.4 convert_element_type.43
  286.8 1.4 convert_element_type.44
  288.2 1.4 convert_element_type.45
  289.7 1.4 convert_element_type.46
  291.1 1.4 convert_element_type.47
  292.6 1.4 convert_element_type.48
  294.0 1.6 convert_element_type.49
  295.6 0.0 copy-done.3
  295.6 0.9 copy.46
  296.5 0.0 copy-done
  296.5 0.3 reshape.210
  296.8 0.0 copy-start.2
  296.8 1.4 copy.45
  298.2 0.0 copy-done.2
  298.2 0.0 copy-start.1
  298.2 0.9 copy.49
  299.0 0.5 copy-done.1
  299.6 0.9 copy.50
  (3 shorter events, 0.0 us)
Async XLA Ops:
  280.7 15.0 %copy-start.3 = (bf16[768,96]{1,0:T(8,128)(2,1)S(1)}, bf16[768,96]{1,0:T(8,128)(2,1)}, u32[]{:S(2)}) copy-start(bf16[768,96]{1,0:T(8,128)(2,1)} %get-tuple-element.45) | copy-start | bytes 442372
  280.7 15.8 %copy-start = (bf16[8,96,768]{2,1,0:T(8,128)(2,1)S(1)}, bf16[8,96,768]{2,1,0:T(8,128)(2,1)}, u32[]{:S(2)}) copy-start(bf16[8,96,768]{2,1,0:T(8,128)(2,1)} %get-tuple-element.35) | copy-start | bytes 3538948
  296.8 1.4 copy-start.2
  298.2 1.4 copy-start.1
